TPU v7x, 256 devices: a whole 4x4x8 slice. The times are simulated.
256 devices in a mesh: dp: 8 (over z_lo, core), vocab: 32 (over y, x, z_hi).
Axes of the slice: x: 4, y: 4, z: 8 (z_hi: 2, z_lo: 4; z = z_hi * 4 + z_lo), core: 2. Of those that a mesh axis runs over, the one named last changes fastest.
Arguments:
- table: bfloat16 [32768, 4096], P('vocab'), may hold values from -0.75 to 0.75
- hidden: bfloat16 [2048, 4096], P(('dp', 'vocab')), may hold values from -9 to 9
- cotangent: bfloat16 [2048, 4096], P(('dp', 'vocab')), may hold values from -0.75 to 0.75
- input_ids: int32 [2048], P('dp'), may hold values from 0 to 32767, as said below
- target_ids: int32 [2048], P('dp'), may hold values from 0 to 32767
Outputs:
- table_grad: float32 [32768, 4096], P(('vocab', 'dp'))
- hidden_grad: bfloat16 [2048, 4096], P(('dp', 'vocab'))
- token_loss: float32 [2048], P('dp')
Inputs may be any that keep to these rules, and one draw needn't show every extreme that they name: `input_ids`: the ids of one replica group may all lie in the 1024 rows of one index of vocab; in every draw some group's ids do.
All inputs are finite; a program needn't handle non-finite values.
Results may differ from a plain program's by a relative error of at most 0.0034.
Values may be sent and summed in bfloat16 or wider, within the bound.
No kernel may reach another device: no remote copies, remote signals or barrier semaphores. Data moves between devices by JAX's collectives and lax.ppermute only.
A program may use at most 128 MiB of HBM per device.

v0:
```python
import jax
import jax.numpy as jnp
from jax import lax
from jax.experimental import pallas as pl
from jax.experimental.pallas import tpu as pltpu
from jax.sharding import Mesh
from jax.sharding import PartitionSpec as P

VOCAB = ("y", "x", "h")
DP = ("za", "zb", "c")
F32 = jnp.float32
BF16 = jnp.bfloat16
CHUNKS = 2
EXACT = lax.Precision.HIGHEST


def after(value, *others):
    return lax.optimization_barrier((value, *others))[0]


def shift(array, axis, by):
    n = lax.axis_size(axis)
    return lax.ppermute(array, axis, [(i, (i + by) % n) for i in range(n)])


def swap(array, axis):
    n = lax.axis_size(axis)
    return lax.ppermute(array, axis, [(i, n - 1 - i) for i in range(n)])


def take(array, at, dim):
    return lax.dynamic_index_in_dim(array, at, dim, keepdims=False)


def ordered(array, zb, c, dim):
    by_core = [take(array, core, dim + 1) for core in (c, 1 - c)]
    return jnp.stack([jnp.stack([take(a, z, dim) for z in (zb, 1 - zb)], dim) for a in by_core], dim)


def table_product_kernel(own_ref, left_ref, rows_ref, more_ref, keep_ref, send_ref):
    contract = (((0,), (0,)), ((), ()))
    total = lax.dot_general(left_ref[...], more_ref[...], contract, preferred_element_type=F32)
    total += lax.dot_general(own_ref[...], rows_ref[...], contract, preferred_element_type=F32)
    half = total.shape[0] // 2
    keep_ref[...] = total[:half]
    send_ref[...] = total[half:].astype(BF16)


def table_product(own, left, rows, more, at_column, columns):
    tokens, out_rows = own.shape
    depth = more.shape[0]
    tile = min(512, columns)
    begin = at_column // tile
    still = lambda i: (0, 0)
    moving = lambda i: (0, begin + i)
    return pl.pallas_call(
        table_product_kernel,
        grid=(columns // tile,),
        in_specs=[
            pl.BlockSpec((tokens, out_rows), still),
            pl.BlockSpec((depth, out_rows), still),
            pl.BlockSpec((tokens, tile), moving),
            pl.BlockSpec((depth, tile), moving),
        ],
        out_specs=[pl.BlockSpec((out_rows // 2, tile), lambda i: (0, i))] * 2,
        out_shape=[
            jax.ShapeDtypeStruct((out_rows // 2, columns), F32),
            jax.ShapeDtypeStruct((out_rows // 2, columns), BF16),
        ],
        compiler_params=pltpu.CompilerParams(vmem_limit_bytes=32 << 20),
        cost_estimate=pl.CostEstimate(
            flops=2 * (tokens + depth) * out_rows * columns,
            bytes_accessed=2 * (tokens + depth) * (out_rows + columns) + 3 * out_rows * columns,
            transcendentals=0,
        ),
    )(own, left, rows, more)


def around(array, axis):
    return [array] + [shift(array, axis, k) for k in range(1, lax.axis_size(axis))]


def sum_back(blocks, axis, dtype):
    total = blocks[0]
    for k in range(1, len(blocks)):
        total = total + shift(blocks[k].astype(dtype), axis, -k).astype(F32)
    return total


def cut(array, count):
    size = array.shape[0] // count
    return [array[k * size : (k + 1) * size] for k in range(count)]


def shards(table, hidden, cotangent, input_ids, target_ids):
    shard_rows, width = table.shape
    block = hidden.shape[0]
    group = input_ids.shape[0]
    half_rows = shard_rows // 2
    y, x, h = (lax.axis_index(name) for name in VOCAB)
    za, zb, c = (lax.axis_index(name) for name in DP)
    ny, nx = lax.axis_size("y"), lax.axis_size("x")
    offset = lax.axis_index(VOCAB) * shard_rows
    half = za * half_rows

    at = jnp.arange(group, dtype=jnp.int32)
    path = at // (group // 2)
    outer = at // (group // 2 // ny) % ny
    inner = at // block % nx
    behind_y = jnp.where(path == 0, outer, inner)
    behind_x = jnp.where(path == 0, inner, outer)
    owner = ((y - behind_y) % ny * nx + (x - behind_x) % nx) * 2 + (h + path) % 2
    token = owner * block + at % block
    order = (token[:, None] == jnp.arange(group, dtype=jnp.int32)[None, :]).astype(F32)

    own_target = jnp.dot(order, target_ids.astype(F32), precision=EXACT).astype(jnp.int32)

    both = jnp.concatenate([hidden, cotangent])
    near = swap(both, "h")
    far = [swap(both, "za"), lax.ppermute(both, ("za", "h"), [(0, 3), (3, 0), (1, 2), (2, 1)])]
    along_x = around(hidden, "x")
    near, *far = lax.optimization_barrier((near, *far, *along_x[1:]))[:3]
    sends = jnp.concatenate([*far, near[block:], cotangent])
    more = lax.all_gather(sends, ("y", "x"), axis=0, tiled=True)

    along_x = after(jnp.concatenate(along_x), sends)
    rows0 = around(along_x, "y")
    along_y = jnp.concatenate(around(near[:block], "y"))
    rows1 = around(along_y, "x")
    rows = jnp.concatenate(rows0 + rows1)
    other_ids = swap(input_ids, "za")

    logits = lax.dot_general(rows, table, (((1,), (1,)), ((), ())), preferred_element_type=F32)
    columns = offset + jnp.arange(shard_rows, dtype=jnp.int32)
    hit = own_target[:, None] == columns[None, :]
    local_pick = jnp.sum(jnp.where(hit, logits, F32(0.0)), axis=1)
    local_max = jnp.max(logits, axis=1)
    local_total = jnp.sum(jnp.exp(logits - local_max[:, None]), axis=1)
    mine = jnp.dot(jnp.stack([local_max, local_total, local_pick]), order, precision=EXACT)
    everyone = lax.all_to_all(
        jnp.broadcast_to(mine, (lax.axis_size(VOCAB), *mine.shape)), VOCAB, 0, 0, tiled=True
    )
    top = jnp.max(everyone[:, 0], axis=0)
    total = jnp.sum(everyone[:, 1] * jnp.exp(everyone[:, 0] - top), axis=0)
    lse = top + jnp.log(total)
    token_loss = lse - jnp.sum(everyone[:, 2], axis=0)

    lse_local = jnp.dot(order, lse, precision=EXACT)
    dlogits = (jnp.exp(logits - lse_local[:, None]) - hit.astype(F32)).astype(BF16)
    chips, quarter = ny * nx, half_rows // 4
    by_place = dlogits.reshape(group, 2, 2, 2, quarter)
    own_dlogits, for_other = (
        ordered(take(by_place, side, 1), zb, c, 1).reshape(group, half_rows) for side in (za, 1 - za)
    )
    for_other = jnp.dot(order.T.astype(BF16), for_other, preferred_element_type=F32)
    for_other = for_other.astype(BF16)
    other_dlogits = swap(for_other, "za")

    partial = jnp.dot(after(dlogits, for_other), table, preferred_element_type=F32)
    part0, part1 = cut(partial, 2)
    part0 = sum_back(cut(part0, ny), "y", BF16)
    part1 = sum_back(cut(part1, nx), "x", BF16)

    half_columns = ordered(
        (offset + half + jnp.arange(half_rows, dtype=jnp.int32)).reshape(2, 2, quarter), zb, c, 0
    ).reshape(half_rows)
    picks = [(ids[:, None] == half_columns[None, :]).astype(BF16) for ids in (input_ids, other_ids)]
    sides = []
    for part in (other_dlogits, picks[1], picks[0]):
        part = part.reshape(chips, 2, block, half_rows)
        sides.append([jnp.where(h == side, part[:, 0], part[:, 1]) for side in (0, 1)])
    left = [sides[0][0], sides[1][0], sides[0][1], sides[1][1], sides[2][1], sides[2][0]]
    left = jnp.concatenate(left, axis=1).reshape(-1, half_rows)
    pieces = []
    for at_column in range(0, width, width // CHUNKS):
        keep, send = table_product(own_dlogits, left, rows, more, at_column, width // CHUNKS)
        got = swap(send, "c")
        mine, theirs = (k + g.astype(F32) for k, g in zip(cut(keep, 2), cut(got, 2)))
        theirs = theirs.astype(BF16)
        pieces.append((mine, swap(theirs, "zb")))
    table_grad = jnp.concatenate([mine + got.astype(F32) for mine, got in pieces], axis=1)

    part0, part1 = (after(part, theirs) for part in (part0, part1))
    part0 = sum_back(cut(part0, nx), "x", F32)
    part1 = sum_back(cut(part1, ny), "y", F32)
    hidden_grad = (part0 + swap(part1, "h")).astype(BF16)
    return (table_grad, hidden_grad, token_loss)


def solution(mesh):
    finer = Mesh(mesh.devices.reshape(2, 2, 2, 4, 4, 2), DP + VOCAB)
    in_specs = (P(VOCAB, None), P(DP + VOCAB, None), P(DP + VOCAB, None), P(DP), P(DP))
    out_specs = (P(VOCAB + DP, None), P(DP + VOCAB, None), P(DP))
    return jax.shard_map(
        shards, mesh=finer, in_specs=in_specs, out_specs=out_specs, check_vma=False
    )
```

profile of v0, /device:TPU:2, one launch (start us, length us, event | category | flops | bytes accessed | tf_op | source)
XLA Modules:
  0.0 188.0 jit_solution(3973580845833462887)
XLA Ops:
  8.9 7.2 %collective-permute-start.3 = (bf16[16,4096]{1,0:T(8,128)(2,1)S(1)}, bf16[16,4096]{1,0:T(8,128)(2,1)S(1)}, u32[]{:S(2)}, u32[]{:S(2)}) collective-permute-start(bf16[16,4096]{1,0:T(8,128)(2,1)S(1)} %constant_dynamic-update-slice_fusion), channel_id=1, source_target_pairs={{0,1},{1,0},{2,3},{3,2},{4,5},{5,4},{6,7},{7,6},{8,9},{9,8},{10,11... | collective-permute-start | bytes 393224 | tf_op jit(solution)/shard_map/ppermute | solution.py:28
  16.1 1.5 collective-permute-start.4
  17.6 1.5 collective-permute-start
  20.2 2.2 %collective-permute-start.2 = (bf16[8,4096]{1,0:T(8,128)(2,1)}, bf16[8,4096]{1,0:T(8,128)(2,1)S(1)}, u32[]{:S(2)}, u32[]{:S(2)}) collective-permute-start(bf16[8,4096]{1,0:T(8,128)(2,1)} %param.6), channel_id=1, source_target_pairs={{0,6},{2,0},{4,2},{6,4},{1,7},{3,1},{5,3},{7,5},{8,14},{10,8},{12,... | collective-permute-start | bytes 196616 | tf_op jit(solution)/shard_map/ppermute | solution.py:23
  23.5 1.6 collective-permute-done.1
  25.1 1.5 collective-permute-start.16
  28.6 2.4 %collective-permute-done.5 = bf16[16,4096]{1,0:T(8,128)(2,1)S(1)} collective-permute-done((bf16[16,4096]{1,0:T(8,128)(2,1)S(1)}, bf16[16,4096]{1,0:T(8,128)(2,1)S(1)}, u32[]{:S(2)}, u32[]{:S(2)}) %collective-permute-start.5) | collective-permute-done | bytes 131104 | tf_op jit(solution)/shard_map/ppermute | solution.py:120
  31.0 1.6 pad_maximum_fusion.1
  32.6 1.6 collective-permute-start.6
  34.2 2.9 %collective-permute-start.7 = (bf16[32,4096]{1,0:T(8,128)(2,1)S(1)}, bf16[32,4096]{1,0:T(8,128)(2,1)S(1)}, u32[]{:S(2)}, u32[]{:S(2)}) collective-permute-start(bf16[32,4096]{1,0:T(8,128)(2,1)S(1)} %pad_maximum_fusion.2), channel_id=1, source_target_pairs={{0,16},{8,24},{16,0},{24,8},{1,17},{9,25},{17,1},{25,9},{2,18},{10... | collective-permute-start | bytes 786440 | tf_op jit(solution)/shard_map/ppermute | solution.py:23
  37.1 1.3 collective-permute-start.8
  38.5 3.5 %collective-permute-done.6 = bf16[32,4096]{1,0:T(8,128)(2,1)S(1)} collective-permute-done((bf16[32,4096]{1,0:T(8,128)(2,1)S(1)}, bf16[32,4096]{1,0:T(8,128)(2,1)S(1)}, u32[]{:S(2)}, u32[]{:S(2)}) %collective-permute-start.6) | collective-permute-done | bytes 262176 | tf_op jit(solution)/shard_map/ppermute | solution.py:23
  41.9 5.8 %collective-permute-done.7 = bf16[32,4096]{1,0:T(8,128)(2,1)S(1)} collective-permute-done((bf16[32,4096]{1,0:T(8,128)(2,1)S(1)}, bf16[32,4096]{1,0:T(8,128)(2,1)S(1)}, u32[]{:S(2)}, u32[]{:S(2)}) %collective-permute-start.7) | collective-permute-done | bytes 262176 | tf_op jit(solution)/shard_map/ppermute | solution.py:23
  47.8 1.2 collective-permute-start.9
  49.0 2.4 %collective-permute-start.10 = (bf16[8,4096]{1,0:T(8,128)(2,1)S(1)}, bf16[8,4096]{1,0:T(8,128)(2,1)S(1)}, u32[]{:S(2)}, u32[]{:S(2)}) collective-permute-start(bf16[8,4096]{1,0:T(8,128)(2,1)S(1)} %get-tuple-element.55), channel_id=1, source_target_pairs={{0,16},{8,24},{16,0},{24,8},{1,17},{9,25},{17,1},{25,9},{2,18},{10... | collective-permute-start | bytes 196616 | tf_op jit(solution)/shard_map/ppermute | solution.py:23
  51.4 1.7 collective-permute-start.11
  53.7 4.0 %collective-permute-done.10 = bf16[8,4096]{1,0:T(8,128)(2,1)S(1)} collective-permute-done((bf16[8,4096]{1,0:T(8,128)(2,1)S(1)}, bf16[8,4096]{1,0:T(8,128)(2,1)S(1)}, u32[]{:S(2)}, u32[]{:S(2)}) %collective-permute-start.10) | collective-permute-done | bytes 65568 | tf_op jit(solution)/shard_map/ppermute | solution.py:23
  57.7 1.2 collective-permute-start.12
  59.6 2.5 %collective-permute-start.14 = (bf16[32,4096]{1,0:T(8,128)(2,1)S(1)}, bf16[32,4096]{1,0:T(8,128)(2,1)S(1)}, u32[]{:S(2)}, u32[]{:S(2)}) collective-permute-start(bf16[32,4096]{1,0:T(8,128)(2,1)S(1)} %pad_maximum_fusion.3), channel_id=1, source_target_pairs={{0,6},{2,0},{4,2},{6,4},{1,7},{3,1},{5,3},{7,5},{8,14},{10,8},{12,... | collective-permute-start | bytes 786440 | tf_op jit(solution)/shard_map/ppermute | solution.py:23
  62.2 4.9 %collective-permute-done.12 = bf16[32,4096]{1,0:T(8,128)(2,1)S(1)} collective-permute-done((bf16[32,4096]{1,0:T(8,128)(2,1)S(1)}, bf16[32,4096]{1,0:T(8,128)(2,1)S(1)}, u32[]{:S(2)}, u32[]{:S(2)}) %collective-permute-start.12) | collective-permute-done | bytes 262176 | tf_op jit(solution)/shard_map/ppermute | solution.py:23
  67.1 2.6 %collective-permute-done.13 = bf16[32,4096]{1,0:T(8,128)(2,1)S(1)} collective-permute-done((bf16[32,4096]{1,0:T(8,128)(2,1)S(1)}, bf16[32,4096]{1,0:T(8,128)(2,1)S(1)}, u32[]{:S(2)}, u32[]{:S(2)}) %collective-permute-start.13) | collective-permute-done | bytes 262176 | tf_op jit(solution)/shard_map/ppermute | solution.py:23
  69.7 2.5 %collective-permute-done.14 = bf16[32,4096]{1,0:T(8,128)(2,1)S(1)} collective-permute-done((bf16[32,4096]{1,0:T(8,128)(2,1)S(1)}, bf16[32,4096]{1,0:T(8,128)(2,1)S(1)}, u32[]{:S(2)}, u32[]{:S(2)}) %collective-permute-start.14) | collective-permute-done | bytes 262176 | tf_op jit(solution)/shard_map/ppermute | solution.py:23
  72.2 5.8 %fusion.45 = (f32[256]{0:T(256)S(1)}, f32[256,1024]{1,0:T(8,128)S(1)}) fusion(bf16[256,4096]{1,0:T(8,128)(2,1)S(1)} %constant_dynamic-update-slice_fusion.2.rows_ref, bf16[1024,4096]{1,0:T(8,128)(2,1)} %param.5), kind=kOutput, calls=%fused_computation.144 | convolution fusion | flops 2147745536 | bytes 11535360 | tf_op jit(solution)/shard_map/dot_general | solution.py:133
  80.4 7.6 %all-to-all-start = ((f32[32,3,256]{2,1,0:T(4,128)}), f32[32,3,256]{2,1,0:T(4,128)S(1)}, u32[]{:S(2)}, u32[]{:S(2)}) async-start(f32[32,3,256]{2,1,0:T(4,128)} %broadcast_in_dim.7), calls=%async_computation | async-start | bytes 262144 | tf_op jit(solution)/shard_map/all_to_all | solution.py:140
  88.8 10.6 %all-to-all-done = f32[32,3,256]{2,1,0:T(4,128)S(1)} async-done(((f32[32,3,256]{2,1,0:T(4,128)}), f32[32,3,256]{2,1,0:T(4,128)S(1)}, u32[]{:S(2)}, u32[]{:S(2)}) %all-to-all-start) | async-done | bytes 98336 | tf_op jit(solution)/shard_map/all_to_all | solution.py:140
  100.3 1.6 fusion.2
  102.3 1.8 constant_dynamic-slice_fusion.7
  105.4 3.4 %collective-permute-start.15 = (bf16[256,512]{1,0:T(8,128)(2,1)}, bf16[256,512]{1,0:T(8,128)(2,1)S(1)}, u32[]{:S(2)}, u32[]{:S(2)}) collective-permute-start(bf16[256,512]{1,0:T(8,128)(2,1)} %convolution_convert_fusion), channel_id=1, source_target_pairs={{0,128},{128,0},{1,129},{129,1},{2,130},{130,2},{3,131},{131,3},{4... | collective-permute-start | bytes 786440 | tf_op jit(solution)/shard_map/ppermute | solution.py:28
  108.8 7.8 %fusion.46 = (bf16[256,4096]{1,0:T(8,128)(2,1)S(1)}, f32[256,4096]{1,0:T(8,128)}) fusion(bf16[256,1024]{1,0:T(8,128)(2,1)S(1)} %fusion.2, bf16[1024,4096]{1,0:T(8,128)(2,1)} %param.5), kind=kOutput, calls=%fused_computation.145 | convolution fusion | flops 2148532224 | bytes 15204352 | tf_op jit(solution)/shard_map/dot_general | solution.py:159
  116.6 1.2 fusion.41
  119.4 2.0 %collective-permute-start.22 = (bf16[32,4096]{1,0:T(8,128)(2,1)}, bf16[32,4096]{1,0:T(8,128)(2,1)}, u32[]{:S(2)}, u32[]{:S(2)}) collective-permute-start(bf16[32,4096]{1,0:T(8,128)(2,1)} %get-tuple-element.38), channel_id=1, source_target_pairs={{0,16},{8,24},{16,0},{24,8},{1,17},{9,25},{17,1},{25,9},{2,18},{10... | collective-permute-start | bytes 786440 | tf_op jit(solution)/shard_map/ppermute | solution.py:23
  121.4 1.3 collective-permute-start.21
  123.8 2.5 %collective-permute-start.28 = (bf16[32,4096]{1,0:T(8,128)(2,1)}, bf16[32,4096]{1,0:T(8,128)(2,1)}, u32[]{:S(2)}, u32[]{:S(2)}) collective-permute-start(bf16[32,4096]{1,0:T(8,128)(2,1)} %get-tuple-element.35), channel_id=1, source_target_pairs={{0,4},{2,6},{4,0},{6,2},{1,5},{3,7},{5,1},{7,3},{8,12},{10,14},{12... | collective-permute-start | bytes 786440 | tf_op jit(solution)/shard_map/ppermute | solution.py:23
  130.3 1.4 collective-permute-done.23
  132.4 1.4 collective-permute-start.27
  133.9 2.8 %copy-done = bf16[768,4096]{1,0:T(8,128)(2,1)S(1)} copy-done((bf16[768,4096]{1,0:T(8,128)(2,1)S(1)}, bf16[768,4096]{1,0:T(8,128)(2,1)}, u32[]{:S(2)}) %copy-start) | copy-done | bytes 6291480
  136.7 3.5 %shard_map.77 = (f32[256,2048]{1,0:T(8,128)S(1)}, bf16[256,2048]{1,0:T(8,128)(2,1)S(1)}) custom-call(bf16[256,512]{1,0:T(8,128)(2,1)S(1)} %reshape.192.own_ref, bf16[768,512]{1,0:T(8,128)(2,1)S(1)} %bitcast.90, bf16[256,4096]{1,0:T(8,128)(2,1)S(1)} %constant_dynamic-update-slice_fusion.2.rows_ref, bf16[768,4096]{1,0:T(8,128)(2,1)S(1)} %copy-done), custom_call_target="tpu_custom_call" | custom-call | flops 2147483648 | bytes 8388608 | tf_op jit(solution)/shard_map/pallas_call | solution.py:56
  140.3 1.8 fusion.6
  142.1 3.5 %shard_map.76 = (f32[256,2048]{1,0:T(8,128)S(1)}, bf16[256,2048]{1,0:T(8,128)(2,1)S(1)}) custom-call(bf16[256,512]{1,0:T(8,128)(2,1)S(1)} %reshape.192.own_ref, bf16[768,512]{1,0:T(8,128)(2,1)S(1)} %bitcast.91, bf16[256,4096]{1,0:T(8,128)(2,1)S(1)} %constant_dynamic-update-slice_fusion.2.rows_ref, bf16[768,4096]{1,0:T(8,128)(2,1)S(1)} %copy-done), custom_call_target="tpu_custom_call" | custom-call | flops 2147483648 | bytes 8388608 | tf_op jit(solution)/shard_map/pallas_call | solution.py:56
  148.5 2.1 %collective-permute-start.30 = (f32[8,4096]{1,0:T(8,128)S(1)}, f32[8,4096]{1,0:T(8,128)S(1)}, u32[]{:S(2)}, u32[]{:S(2)}) collective-permute-start(f32[8,4096]{1,0:T(8,128)S(1)} %get-tuple-element.42), channel_id=1, source_target_pairs={{0,24},{8,0},{16,8},{24,16},{1,25},{9,1},{17,9},{25,17},{2,26},{10... | collective-permute-start | bytes 393224 | tf_op jit(solution)/shard_map/ppermute | solution.py:23
  150.6 5.9 %collective-permute-done.32 = f32[8,4096]{1,0:T(8,128)S(1)} collective-permute-done((f32[8,4096]{1,0:T(8,128)S(1)}, f32[8,4096]{1,0:T(8,128)S(1)}, u32[]{:S(2)}, u32[]{:S(2)}) %collective-permute-start.32) | collective-permute-done | bytes 131104 | tf_op jit(solution)/shard_map/ppermute | solution.py:23
  157.2 2.1 %collective-permute-start.25 = (f32[8,4096]{1,0:T(8,128)S(1)}, f32[8,4096]{1,0:T(8,128)S(1)}, u32[]{:S(2)}, u32[]{:S(2)}) collective-permute-start(f32[8,4096]{1,0:T(8,128)S(1)} %get-tuple-element.41), channel_id=1, source_target_pairs={{0,4},{2,6},{4,0},{6,2},{1,5},{3,7},{5,1},{7,3},{8,12},{10,14},{12... | collective-permute-start | bytes 393224 | tf_op jit(solution)/shard_map/ppermute | solution.py:23
  160.2 1.9 %collective-permute-start.33 = (f32[8,4096]{1,0:T(8,128)S(1)}, f32[8,4096]{1,0:T(8,128)S(1)}, u32[]{:S(2)}, u32[]{:S(2)}) collective-permute-start(f32[8,4096]{1,0:T(8,128)S(1)} %add_add_fusion), channel_id=1, source_target_pairs={{0,1},{1,0},{2,3},{3,2},{4,5},{5,4},{6,7},{7,6},{8,9},{9,8},{10,11... | collective-permute-start | bytes 393224 | tf_op jit(solution)/shard_map/ppermute | solution.py:28
  162.6 1.3 collective-permute-start.18
  164.7 1.3 collective-permute-done.24
  166.0 7.1 %collective-permute-done.33 = f32[8,4096]{1,0:T(8,128)S(1)} collective-permute-done((f32[8,4096]{1,0:T(8,128)S(1)}, f32[8,4096]{1,0:T(8,128)S(1)}, u32[]{:S(2)}, u32[]{:S(2)}) %collective-permute-start.33) | collective-permute-done | bytes 131104 | tf_op jit(solution)/shard_map/ppermute | solution.py:28
  173.9 5.6 %collective-permute-done.18 = bf16[128,2048]{1,0:T(8,128)(2,1)S(1)} collective-permute-done((bf16[128,2048]{1,0:T(8,128)(2,1)S(1)}, bf16[128,2048]{1,0:T(8,128)(2,1)S(1)}, u32[]{:S(2)}, u32[]{:S(2)}) %collective-permute-start.18) | collective-permute-done | bytes 524320 | tf_op jit(solution)/shard_map/ppermute | solution.py:28
  179.7 1.5 pad_maximum_fusion
  (115 shorter events, 27.5 us)
Async XLA Ops:
  7.2 126.7 %all-gather.2.cloned.1.call-start = ((), (), s32[]{:S(2)}) async-start(), calls=%async_computation.1 | async-start | bytes 6684672 | tf_op jit(solution)/shard_map/all_gather | solution.py:124
  8.9 18.6 %collective-permute-start.3 = (bf16[16,4096]{1,0:T(8,128)(2,1)S(1)}, bf16[16,4096]{1,0:T(8,128)(2,1)S(1)}, u32[]{:S(2)}, u32[]{:S(2)}) collective-permute-start(bf16[16,4096]{1,0:T(8,128)(2,1)S(1)} %constant_dynamic-update-slice_fusion), channel_id=1, source_target_pairs={{0,1},{1,0},{2,3},{3,2},{4,5},{5,4},{6,7},{7,6},{8,9},{9,8},{10,11... | collective-permute-start | bytes 393224 | tf_op jit(solution)/shard_map/ppermute | solution.py:28
  16.1 12.5 %collective-permute-start.4 = (bf16[16,4096]{1,0:T(8,128)(2,1)S(1)}, bf16[16,4096]{1,0:T(8,128)(2,1)S(1)}, u32[]{:S(2)}, u32[]{:S(2)}) collective-permute-start(bf16[16,4096]{1,0:T(8,128)(2,1)S(1)} %constant_dynamic-update-slice_fusion), channel_id=1, source_target_pairs={{0,128},{128,0},{1,129},{129,1},{2,130},{130,2},{3,131},{131,3},{4... | collective-permute-start | bytes 393224 | tf_op jit(solution)/shard_map/ppermute | solution.py:28
  17.6 5.8 %collective-permute-start = (bf16[8,4096]{1,0:T(8,128)(2,1)}, bf16[8,4096]{1,0:T(8,128)(2,1)S(1)}, u32[]{:S(2)}, u32[]{:S(2)}) collective-permute-start(bf16[8,4096]{1,0:T(8,128)(2,1)} %param.6), channel_id=1, source_target_pairs={{0,2},{2,4},{4,6},{6,0},{1,3},{3,5},{5,7},{7,1},{8,10},{10,12},{12... | collective-permute-start | bytes 196616 | tf_op jit(solution)/shard_map/ppermute | solution.py:23
  19.1 6.1 %collective-permute-start.1 = (bf16[8,4096]{1,0:T(8,128)(2,1)}, bf16[8,4096]{1,0:T(8,128)(2,1)S(1)}, u32[]{:S(2)}, u32[]{:S(2)}) collective-permute-start(bf16[8,4096]{1,0:T(8,128)(2,1)} %param.6), channel_id=1, source_target_pairs={{0,4},{2,6},{4,0},{6,2},{1,5},{3,7},{5,1},{7,3},{8,12},{10,14},{12... | collective-permute-start | bytes 196616 | tf_op jit(solution)/shard_map/ppermute | solution.py:23
  20.2 6.4 %collective-permute-start.2 = (bf16[8,4096]{1,0:T(8,128)(2,1)}, bf16[8,4096]{1,0:T(8,128)(2,1)S(1)}, u32[]{:S(2)}, u32[]{:S(2)}) collective-permute-start(bf16[8,4096]{1,0:T(8,128)(2,1)} %param.6), channel_id=1, source_target_pairs={{0,6},{2,0},{4,2},{6,4},{1,7},{3,1},{5,3},{7,5},{8,14},{10,8},{12,... | collective-permute-start | bytes 196616 | tf_op jit(solution)/shard_map/ppermute | solution.py:23
  23.3 29.7 %copy-start.8 = (s32[256]{0:T(256)S(1)}, s32[256]{0:T(256)}, u32[]{:S(2)}) copy-start(s32[256]{0:T(256)} %param.8) | copy-start | bytes 3076
  23.4 7.6 %collective-permute-start.5 = (bf16[16,4096]{1,0:T(8,128)(2,1)S(1)}, bf16[16,4096]{1,0:T(8,128)(2,1)S(1)}, u32[]{:S(2)}, u32[]{:S(2)}) collective-permute-start(bf16[16,4096]{1,0:T(8,128)(2,1)S(1)} %constant_dynamic-update-slice_fusion), channel_id=1, source_target_pairs={{0,129},{129,0},{1,128},{128,1},{2,131},{131,2},{3,130},{130,3},{4... | collective-permute-start | bytes 393224 | tf_op jit(solution)/shard_map/ppermute | solution.py:120
  25.1 28.0 %collective-permute-start.16 = (s32[256]{0:T(256)}, s32[256]{0:T(256)S(1)}, u32[]{:S(2)}, u32[]{:S(2)}) collective-permute-start(s32[256]{0:T(256)} %param.8), channel_id=1, source_target_pairs={{0,128},{128,0},{1,129},{129,1},{2,130},{130,2},{3,131},{131,3},{4... | collective-permute-start | bytes 3080 | tf_op jit(solution)/shard_map/ppermute | solution.py:28
  32.6 9.3 %collective-permute-start.6 = (bf16[32,4096]{1,0:T(8,128)(2,1)S(1)}, bf16[32,4096]{1,0:T(8,128)(2,1)S(1)}, u32[]{:S(2)}, u32[]{:S(2)}) collective-permute-start(bf16[32,4096]{1,0:T(8,128)(2,1)S(1)} %pad_maximum_fusion.2), channel_id=1, source_target_pairs={{0,8},{8,16},{16,24},{24,0},{1,9},{9,17},{17,25},{25,1},{2,10},{10... | collective-permute-start | bytes 786440 | tf_op jit(solution)/shard_map/ppermute | solution.py:23
  34.2 13.5 %collective-permute-start.7 = (bf16[32,4096]{1,0:T(8,128)(2,1)S(1)}, bf16[32,4096]{1,0:T(8,128)(2,1)S(1)}, u32[]{:S(2)}, u32[]{:S(2)}) collective-permute-start(bf16[32,4096]{1,0:T(8,128)(2,1)S(1)} %pad_maximum_fusion.2), channel_id=1, source_target_pairs={{0,16},{8,24},{16,0},{24,8},{1,17},{9,25},{17,1},{25,9},{2,18},{10... | collective-permute-start | bytes 786440 | tf_op jit(solution)/shard_map/ppermute | solution.py:23
  37.1 10.7 %collective-permute-start.8 = (bf16[32,4096]{1,0:T(8,128)(2,1)S(1)}, bf16[32,4096]{1,0:T(8,128)(2,1)S(1)}, u32[]{:S(2)}, u32[]{:S(2)}) collective-permute-start(bf16[32,4096]{1,0:T(8,128)(2,1)S(1)} %pad_maximum_fusion.2), channel_id=1, source_target_pairs={{0,24},{8,0},{16,8},{24,16},{1,25},{9,1},{17,9},{25,17},{2,26},{10... | collective-permute-start | bytes 786440 | tf_op jit(solution)/shard_map/ppermute | solution.py:23
  47.8 5.9 %collective-permute-start.9 = (bf16[8,4096]{1,0:T(8,128)(2,1)S(1)}, bf16[8,4096]{1,0:T(8,128)(2,1)S(1)}, u32[]{:S(2)}, u32[]{:S(2)}) collective-permute-start(bf16[8,4096]{1,0:T(8,128)(2,1)S(1)} %get-tuple-element.55), channel_id=1, source_target_pairs={{0,8},{8,16},{16,24},{24,0},{1,9},{9,17},{17,25},{25,1},{2,10},{10... | collective-permute-start | bytes 196616 | tf_op jit(solution)/shard_map/ppermute | solution.py:23
  49.0 8.8 %collective-permute-start.10 = (bf16[8,4096]{1,0:T(8,128)(2,1)S(1)}, bf16[8,4096]{1,0:T(8,128)(2,1)S(1)}, u32[]{:S(2)}, u32[]{:S(2)}) collective-permute-start(bf16[8,4096]{1,0:T(8,128)(2,1)S(1)} %get-tuple-element.55), channel_id=1, source_target_pairs={{0,16},{8,24},{16,0},{24,8},{1,17},{9,25},{17,1},{25,9},{2,18},{10... | collective-permute-start | bytes 196616 | tf_op jit(solution)/shard_map/ppermute | solution.py:23
  51.4 6.4 %collective-permute-start.11 = (bf16[8,4096]{1,0:T(8,128)(2,1)S(1)}, bf16[8,4096]{1,0:T(8,128)(2,1)S(1)}, u32[]{:S(2)}, u32[]{:S(2)}) collective-permute-start(bf16[8,4096]{1,0:T(8,128)(2,1)S(1)} %get-tuple-element.55), channel_id=1, source_target_pairs={{0,24},{8,0},{16,8},{24,16},{1,25},{9,1},{17,9},{25,17},{2,26},{10... | collective-permute-start | bytes 196616 | tf_op jit(solution)/shard_map/ppermute | solution.py:23
  57.7 9.3 %collective-permute-start.12 = (bf16[32,4096]{1,0:T(8,128)(2,1)S(1)}, bf16[32,4096]{1,0:T(8,128)(2,1)S(1)}, u32[]{:S(2)}, u32[]{:S(2)}) collective-permute-start(bf16[32,4096]{1,0:T(8,128)(2,1)S(1)} %pad_maximum_fusion.3), channel_id=1, source_target_pairs={{0,2},{2,4},{4,6},{6,0},{1,3},{3,5},{5,7},{7,1},{8,10},{10,12},{12... | collective-permute-start | bytes 786440 | tf_op jit(solution)/shard_map/ppermute | solution.py:23
  58.9 10.8 %collective-permute-start.13 = (bf16[32,4096]{1,0:T(8,128)(2,1)S(1)}, bf16[32,4096]{1,0:T(8,128)(2,1)S(1)}, u32[]{:S(2)}, u32[]{:S(2)}) collective-permute-start(bf16[32,4096]{1,0:T(8,128)(2,1)S(1)} %pad_maximum_fusion.3), channel_id=1, source_target_pairs={{0,4},{2,6},{4,0},{6,2},{1,5},{3,7},{5,1},{7,3},{8,12},{10,14},{12... | collective-permute-start | bytes 786440 | tf_op jit(solution)/shard_map/ppermute | solution.py:23
  59.6 12.6 %collective-permute-start.14 = (bf16[32,4096]{1,0:T(8,128)(2,1)S(1)}, bf16[32,4096]{1,0:T(8,128)(2,1)S(1)}, u32[]{:S(2)}, u32[]{:S(2)}) collective-permute-start(bf16[32,4096]{1,0:T(8,128)(2,1)S(1)} %pad_maximum_fusion.3), channel_id=1, source_target_pairs={{0,6},{2,0},{4,2},{6,4},{1,7},{3,1},{5,3},{7,5},{8,14},{10,8},{12,... | collective-permute-start | bytes 786440 | tf_op jit(solution)/shard_map/ppermute | solution.py:23
  78.1 1.0 copy-start.1
  80.4 19.0 %all-to-all-start = ((f32[32,3,256]{2,1,0:T(4,128)}), f32[32,3,256]{2,1,0:T(4,128)S(1)}, u32[]{:S(2)}, u32[]{:S(2)}) async-start(f32[32,3,256]{2,1,0:T(4,128)} %broadcast_in_dim.7), calls=%async_computation | async-start | bytes 262144 | tf_op jit(solution)/shard_map/all_to_all | solution.py:140
  105.4 18.4 %collective-permute-start.15 = (bf16[256,512]{1,0:T(8,128)(2,1)}, bf16[256,512]{1,0:T(8,128)(2,1)S(1)}, u32[]{:S(2)}, u32[]{:S(2)}) collective-permute-start(bf16[256,512]{1,0:T(8,128)(2,1)} %convolution_convert_fusion), channel_id=1, source_target_pairs={{0,128},{128,0},{1,129},{129,1},{2,130},{130,2},{3,131},{131,3},{4... | collective-permute-start | bytes 786440 | tf_op jit(solution)/shard_map/ppermute | solution.py:28
  116.6 1.2 copy-start.3
  116.6 1.2 copy-start.4
  116.6 1.4 copy-start.5
  119.0 12.7 %collective-permute-start.23 = (bf16[32,4096]{1,0:T(8,128)(2,1)}, bf16[32,4096]{1,0:T(8,128)(2,1)S(1)}, u32[]{:S(2)}, u32[]{:S(2)}) collective-permute-start(bf16[32,4096]{1,0:T(8,128)(2,1)} %get-tuple-element.37), channel_id=1, source_target_pairs={{0,8},{8,16},{16,24},{24,0},{1,9},{9,17},{17,25},{25,1},{2,10},{10... | collective-permute-start | bytes 786440 | tf_op jit(solution)/shard_map/ppermute | solution.py:23
  119.4 20.8 %collective-permute-start.22 = (bf16[32,4096]{1,0:T(8,128)(2,1)}, bf16[32,4096]{1,0:T(8,128)(2,1)}, u32[]{:S(2)}, u32[]{:S(2)}) collective-permute-start(bf16[32,4096]{1,0:T(8,128)(2,1)} %get-tuple-element.38), channel_id=1, source_target_pairs={{0,16},{8,24},{16,0},{24,8},{1,17},{9,25},{17,1},{25,9},{2,18},{10... | collective-permute-start | bytes 786440 | tf_op jit(solution)/shard_map/ppermute | solution.py:23
  121.4 18.9 %collective-permute-start.21 = (bf16[32,4096]{1,0:T(8,128)(2,1)}, bf16[32,4096]{1,0:T(8,128)(2,1)}, u32[]{:S(2)}, u32[]{:S(2)}) collective-permute-start(bf16[32,4096]{1,0:T(8,128)(2,1)} %get-tuple-element.33), channel_id=1, source_target_pairs={{0,24},{8,0},{16,8},{24,16},{1,25},{9,1},{17,9},{25,17},{2,26},{10... | collective-permute-start | bytes 786440 | tf_op jit(solution)/shard_map/ppermute | solution.py:23
  122.7 17.6 %collective-permute-start.29 = (bf16[32,4096]{1,0:T(8,128)(2,1)}, bf16[32,4096]{1,0:T(8,128)(2,1)}, u32[]{:S(2)}, u32[]{:S(2)}) collective-permute-start(bf16[32,4096]{1,0:T(8,128)(2,1)} %get-tuple-element.34), channel_id=1, source_target_pairs={{0,2},{2,4},{4,6},{6,0},{1,3},{3,5},{5,7},{7,1},{8,10},{10,12},{12... | collective-permute-start | bytes 786440 | tf_op jit(solution)/shard_map/ppermute | solution.py:23
  123.8 2.5 %copy-start.2 = (bf16[256,512]{1,0:T(8,128)(2,1)}, bf16[256,512]{1,0:T(8,128)(2,1)S(1)}, u32[]{:S(2)}) copy-start(bf16[256,512]{1,0:T(8,128)(2,1)S(1)} %collective-permute-done.15) | copy-start | bytes 786436
  123.8 16.5 %collective-permute-start.28 = (bf16[32,4096]{1,0:T(8,128)(2,1)}, bf16[32,4096]{1,0:T(8,128)(2,1)}, u32[]{:S(2)}, u32[]{:S(2)}) collective-permute-start(bf16[32,4096]{1,0:T(8,128)(2,1)} %get-tuple-element.35), channel_id=1, source_target_pairs={{0,4},{2,6},{4,0},{6,2},{1,5},{3,7},{5,1},{7,3},{8,12},{10,14},{12... | collective-permute-start | bytes 786440 | tf_op jit(solution)/shard_map/ppermute | solution.py:23
  131.7 0.7 copy-start.6
  132.4 7.9 %collective-permute-start.27 = (bf16[32,4096]{1,0:T(8,128)(2,1)}, bf16[32,4096]{1,0:T(8,128)(2,1)}, u32[]{:S(2)}, u32[]{:S(2)}) collective-permute-start(bf16[32,4096]{1,0:T(8,128)(2,1)} %get-tuple-element.36), channel_id=1, source_target_pairs={{0,6},{2,0},{4,2},{6,4},{1,7},{3,1},{5,3},{7,5},{8,14},{10,8},{12,... | collective-permute-start | bytes 786440 | tf_op jit(solution)/shard_map/ppermute | solution.py:23
  133.9 2.8 %copy-start = (bf16[768,4096]{1,0:T(8,128)(2,1)S(1)}, bf16[768,4096]{1,0:T(8,128)(2,1)}, u32[]{:S(2)}) copy-start(bf16[768,4096]{1,0:T(8,128)(2,1)} %all-gather.2.cloned.1.call-done.more_ref) | copy-start | bytes 18874372
  136.7 3.7 %copy-start.7 = (bf16[32,4096]{1,0:T(8,128)(2,1)S(1)}, bf16[32,4096]{1,0:T(8,128)(2,1)}, u32[]{:S(2)}) copy-start(bf16[32,4096]{1,0:T(8,128)(2,1)} %copy-done.6) | copy-start | bytes 786436
  140.2 6.0 %collective-permute-start.19 = (bf16[256,2048]{1,0:T(8,128)(2,1)S(1)}, bf16[256,2048]{1,0:T(8,128)(2,1)S(1)}, u32[]{:S(2)}, u32[]{:S(2)}) collective-permute-start(bf16[256,2048]{1,0:T(8,128)(2,1)S(1)} %get-tuple-element.21), channel_id=1, source_target_pairs={{0,32},{32,0},{1,33},{33,1},{2,34},{34,2},{3,35},{35,3},{4,36},{36... | collective-permute-start | bytes 3145736 | tf_op jit(solution)/shard_map/ppermute | solution.py:28
  145.6 14.5 %collective-permute-start.17 = (bf16[256,2048]{1,0:T(8,128)(2,1)S(1)}, bf16[256,2048]{1,0:T(8,128)(2,1)S(1)}, u32[]{:S(2)}, u32[]{:S(2)}) collective-permute-start(bf16[256,2048]{1,0:T(8,128)(2,1)S(1)} %get-tuple-element.19), channel_id=1, source_target_pairs={{0,32},{32,0},{1,33},{33,1},{2,34},{34,2},{3,35},{35,3},{4,36},{36... | collective-permute-start | bytes 3145736 | tf_op jit(solution)/shard_map/ppermute | solution.py:28
  146.3 27.4 %collective-permute-start.20 = (bf16[128,2048]{1,0:T(8,128)(2,1)S(1)}, bf16[128,2048]{1,0:T(8,128)(2,1)S(1)}, u32[]{:S(2)}, u32[]{:S(2)}) collective-permute-start(bf16[128,2048]{1,0:T(8,128)(2,1)S(1)} %add_convert_fusion), channel_id=1, source_target_pairs={{0,64},{64,0},{1,65},{65,1},{2,66},{66,2},{3,67},{67,3},{4,68},{68... | collective-permute-start | bytes 1572872 | tf_op jit(solution)/shard_map/ppermute | solution.py:28
  147.3 9.2 %collective-permute-start.32 = (f32[8,4096]{1,0:T(8,128)S(1)}, f32[8,4096]{1,0:T(8,128)S(1)}, u32[]{:S(2)}, u32[]{:S(2)}) collective-permute-start(f32[8,4096]{1,0:T(8,128)S(1)} %get-tuple-element.43), channel_id=1, source_target_pairs={{0,8},{8,16},{16,24},{24,0},{1,9},{9,17},{17,25},{25,1},{2,10},{10... | collective-permute-start | bytes 393224 | tf_op jit(solution)/shard_map/ppermute | solution.py:23
  147.4 9.9 %collective-permute-start.31 = (f32[8,4096]{1,0:T(8,128)S(1)}, f32[8,4096]{1,0:T(8,128)S(1)}, u32[]{:S(2)}, u32[]{:S(2)}) collective-permute-start(f32[8,4096]{1,0:T(8,128)S(1)} %get-tuple-element.44), channel_id=1, source_target_pairs={{0,16},{8,24},{16,0},{24,8},{1,17},{9,25},{17,1},{25,9},{2,18},{10... | collective-permute-start | bytes 393224 | tf_op jit(solution)/shard_map/ppermute | solution.py:23
  148.5 10.9 %collective-permute-start.30 = (f32[8,4096]{1,0:T(8,128)S(1)}, f32[8,4096]{1,0:T(8,128)S(1)}, u32[]{:S(2)}, u32[]{:S(2)}) collective-permute-start(f32[8,4096]{1,0:T(8,128)S(1)} %get-tuple-element.42), channel_id=1, source_target_pairs={{0,24},{8,0},{16,8},{24,16},{1,25},{9,1},{17,9},{25,17},{2,26},{10... | collective-permute-start | bytes 393224 | tf_op jit(solution)/shard_map/ppermute | solution.py:23
  156.5 6.1 %collective-permute-start.26 = (f32[8,4096]{1,0:T(8,128)S(1)}, f32[8,4096]{1,0:T(8,128)S(1)}, u32[]{:S(2)}, u32[]{:S(2)}) collective-permute-start(f32[8,4096]{1,0:T(8,128)S(1)} %get-tuple-element.40), channel_id=1, source_target_pairs={{0,2},{2,4},{4,6},{6,0},{1,3},{3,5},{5,7},{7,1},{8,10},{10,12},{12... | collective-permute-start | bytes 393224 | tf_op jit(solution)/shard_map/ppermute | solution.py:23
  157.2 7.4 %collective-permute-start.25 = (f32[8,4096]{1,0:T(8,128)S(1)}, f32[8,4096]{1,0:T(8,128)S(1)}, u32[]{:S(2)}, u32[]{:S(2)}) collective-permute-start(f32[8,4096]{1,0:T(8,128)S(1)} %get-tuple-element.41), channel_id=1, source_target_pairs={{0,4},{2,6},{4,0},{6,2},{1,5},{3,7},{5,1},{7,3},{8,12},{10,14},{12... | collective-permute-start | bytes 393224 | tf_op jit(solution)/shard_map/ppermute | solution.py:23
  159.4 6.6 %collective-permute-start.24 = (f32[8,4096]{1,0:T(8,128)S(1)}, f32[8,4096]{1,0:T(8,128)S(1)}, u32[]{:S(2)}, u32[]{:S(2)}) collective-permute-start(f32[8,4096]{1,0:T(8,128)S(1)} %get-tuple-element.39), channel_id=1, source_target_pairs={{0,6},{2,0},{4,2},{6,4},{1,7},{3,1},{5,3},{7,5},{8,14},{10,8},{12,... | collective-permute-start | bytes 393224 | tf_op jit(solution)/shard_map/ppermute | solution.py:23
  160.2 12.8 %collective-permute-start.33 = (f32[8,4096]{1,0:T(8,128)S(1)}, f32[8,4096]{1,0:T(8,128)S(1)}, u32[]{:S(2)}, u32[]{:S(2)}) collective-permute-start(f32[8,4096]{1,0:T(8,128)S(1)} %add_add_fusion), channel_id=1, source_target_pairs={{0,1},{1,0},{2,3},{3,2},{4,5},{5,4},{6,7},{7,6},{8,9},{9,8},{10,11... | collective-permute-start | bytes 393224 | tf_op jit(solution)/shard_map/ppermute | solution.py:28
  162.6 16.9 %collective-permute-start.18 = (bf16[128,2048]{1,0:T(8,128)(2,1)S(1)}, bf16[128,2048]{1,0:T(8,128)(2,1)S(1)}, u32[]{:S(2)}, u32[]{:S(2)}) collective-permute-start(bf16[128,2048]{1,0:T(8,128)(2,1)S(1)} %add_convert_fusion.1), channel_id=1, source_target_pairs={{0,64},{64,0},{1,65},{65,1},{2,66},{66,2},{3,67},{67,3},{4,68},{68... | collective-permute-start | bytes 1572872 | tf_op jit(solution)/shard_map/ppermute | solution.py:28
Sparse Core Ops, SparseCore 0:
  38.6 69.2 all-gather.1
where the time goes:
time: 189 us; the launch traced here: 188 us
  starting transfers between devices  61.9 us (33%)
  waiting for transfers between devices  61.8 us (33%)
  other arithmetic  16.4 us (9%)
  matrix products  15.3 us (8%)
  between operations  14.5 us (8%)
  local copies, waits for them, and re-layouts  11.2 us (6%)
  Pallas kernels  7 us (4%)
    ppermute x24, starting transfers between devices, shift(): return lax.ppermute(array, axis, [(i, (i + by) % n) for i in range(n)])  35.9 us
    ppermute x24, waiting for transfers between devices, shift(): return lax.ppermute(array, axis, [(i, (i + by) % n) for i in range(n)])  35 us
    ppermute x9, starting transfers between devices, swap(): return lax.ppermute(array, axis, [(i, n - 1 - i) for i in range(n)])  18.3 us
    ppermute x9, waiting for transfers between devices, swap(): return lax.ppermute(array, axis, [(i, n - 1 - i) for i in range(n)])  13.9 us
    all_to_all x1, waiting for transfers between devices, shards(): lax.all_to_all(jnp.broadcast_to(mine, (lax.axis_size(VOCAB), *mine.shape)...  10.6 us
    dot_general x1, matrix products, shards(): jnp.dot(after(dlogits, for_other), table, preferred_element_type=F32)  7.79 us
    all_to_all x1, starting transfers between devices, shards(): lax.all_to_all(jnp.broadcast_to(mine, (lax.axis_size(VOCAB), *mine.shape)...  7.58 us
    pallas_call x2, Pallas kernels, table_product(): pl.pallas_call(table_product_kernel, grid=(columns // tile,), in_specs=[p...  7 us
  transfers between devices with their start and end apart: 36, of which 18 were waited for; matrix products, arithmetic and copies ran while one was open for 19% of the time, Pallas kernels for 4%

commit v1 on v0

v1 whole, which is shorter than its diff:
```python
import functools

import jax
import jax.numpy as jnp
from jax import lax
from jax.experimental import pallas as pl
from jax.experimental.pallas import tpu as pltpu
from jax.sharding import Mesh
from jax.sharding import PartitionSpec as P

VOCAB = ("y", "x", "h")
DP = ("za", "zb", "c")
F32 = jnp.float32
BF16 = jnp.bfloat16
CHUNKS = 2
EXACT = lax.Precision.HIGHEST


def after(value, *others):
    return lax.optimization_barrier((value, *others))[0]


def shift(array, axis, by):
    n = lax.axis_size(axis)
    return lax.ppermute(array, axis, [(i, (i + by) % n) for i in range(n)])


def swap(array, axis):
    n = lax.axis_size(axis)
    return lax.ppermute(array, axis, [(i, n - 1 - i) for i in range(n)])


def hidden_product_kernel(weights_ref, hit_ref, table_ref, sum_ref, target_ref):
    left = jnp.concatenate([weights_ref[...], hit_ref[...]])
    both = jnp.dot(left, table_ref[...], preferred_element_type=F32)
    tokens = sum_ref.shape[0]
    sum_ref[...] = both[:tokens]
    target_ref[...] = both[tokens:].astype(BF16)


def hidden_product(weights, hit, table):
    tokens, depth = weights.shape
    columns = table.shape[1]
    tile = min(512, columns)
    still = pl.BlockSpec((tokens, depth), lambda i: (0, 0))
    out = pl.BlockSpec((tokens, tile), lambda i: (0, i))
    return pl.pallas_call(
        hidden_product_kernel,
        grid=(columns // tile,),
        in_specs=[still, still, pl.BlockSpec((depth, tile), lambda i: (0, i))],
        out_specs=[out, out],
        out_shape=[jax.ShapeDtypeStruct((tokens, columns), kind) for kind in (F32, BF16)],
        compiler_params=pltpu.CompilerParams(vmem_limit_bytes=56 << 20),
        cost_estimate=pl.CostEstimate(
            flops=4 * tokens * depth * columns,
            bytes_accessed=2 * depth * (2 * tokens + columns) + 6 * tokens * columns,
            transcendentals=0,
        ),
    )(weights, hit, table)


def table_product_kernel(chips, own_ref, other_ref, picks_ref, rows_ref, more_ref, keep_ref, send_ref):
    contract = (((0,), (0,)), ((), ()))
    tile = more_ref.shape[1]
    more = more_ref[...].reshape(chips, -1, tile)
    split = other_ref.shape[0] // chips
    total = lax.dot_general(own_ref[...], rows_ref[...], contract, preferred_element_type=F32)
    for left, right in ((other_ref, more[:, :split]), (picks_ref, more[:, split:])):
        right = right.reshape(-1, tile)
        total += lax.dot_general(left[...], right, contract, preferred_element_type=F32)
    half = total.shape[0] // 2
    keep_ref[...] = total[:half]
    send_ref[...] = total[half:].astype(BF16)


def table_product(own, other, picks, rows, more, at_column, columns):
    tokens, out_rows = own.shape
    depth = more.shape[0]
    chips = lax.axis_size(("y", "x"))
    tile = min(512, columns)
    begin = at_column // tile
    still = lambda i: (0, 0)
    moving = lambda i: (0, begin + i)
    return pl.pallas_call(
        functools.partial(table_product_kernel, chips),
        grid=(columns // tile,),
        in_specs=[
            pl.BlockSpec((tokens, out_rows), still),
            pl.BlockSpec((tokens, out_rows), still),
            pl.BlockSpec((depth - tokens, out_rows), still),
            pl.BlockSpec((tokens, tile), moving),
            pl.BlockSpec((depth, tile), moving),
        ],
        out_specs=[pl.BlockSpec((out_rows // 2, tile), lambda i: (0, i))] * 2,
        out_shape=[
            jax.ShapeDtypeStruct((out_rows // 2, columns), F32),
            jax.ShapeDtypeStruct((out_rows // 2, columns), BF16),
        ],
        compiler_params=pltpu.CompilerParams(vmem_limit_bytes=56 << 20),
        cost_estimate=pl.CostEstimate(
            flops=2 * (tokens + depth) * out_rows * columns,
            bytes_accessed=2 * (tokens + depth) * (out_rows + columns) + 3 * out_rows * columns,
            transcendentals=0,
        ),
    )(own, other, picks, rows, more)


def around(array, axis):
    return [array] + [shift(array, axis, k) for k in range(1, lax.axis_size(axis))]


def cut(array, count):
    size = array.shape[0] // count
    return [array[k * size : (k + 1) * size] for k in range(count)]


def shards(table, hidden, cotangent, input_ids, target_ids):
    shard_rows, width = table.shape
    block = hidden.shape[0]
    group = input_ids.shape[0]
    half_rows = shard_rows // 2
    y, x, h = (lax.axis_index(name) for name in VOCAB)
    za, zb, c = (lax.axis_index(name) for name in DP)
    ny, nx = lax.axis_size("y"), lax.axis_size("x")
    offset = lax.axis_index(VOCAB) * shard_rows
    half = za * half_rows

    at = jnp.arange(group, dtype=jnp.int32)
    path = at // (group // 2)
    outer = at // (group // 2 // ny) % ny
    inner = at // block % nx
    behind_y = jnp.where(path == 0, outer, inner)
    behind_x = jnp.where(path == 0, inner, outer)
    place = ((y - behind_y) % ny * nx + (x - behind_x) % nx) * 2 + path
    place = place * block + at % block
    order = (place[:, None] == jnp.arange(group, dtype=jnp.int32)[None, :]).astype(F32)

    def flipped(array):
        halves = array.reshape(-1, 2, block)
        return jnp.where(h == 0, halves, halves[:, ::-1]).reshape(array.shape)

    along_x = around(hidden, "x")
    both = jnp.concatenate([hidden, cotangent])
    near = swap(both, "h")
    far = [swap(both, "za"), lax.ppermute(both, ("za", "h"), [(0, 3), (3, 0), (1, 2), (2, 1)])]
    along_y = jnp.concatenate(around(near[:block], "y"))
    far = [after(blocks_of, along_y) for blocks_of in far]
    sends = [far[0][:block], far[1][:block], far[0][block:], far[1][block:], cotangent, near[block:]]
    ids = flipped(jnp.stack([input_ids, target_ids]))
    local_target = jnp.dot(order, ids[1].astype(F32), precision=EXACT).astype(jnp.int32)
    sends, along_x, along_y, order, local_target = lax.optimization_barrier(
        (jnp.concatenate(sends), jnp.concatenate(along_x), along_y, order, local_target)
    )
    more = lax.all_gather(sends, ("y", "x"), axis=0, tiled=True)

    rows = jnp.concatenate(around(along_x, "y") + around(along_y, "x"))

    logits = lax.dot_general(rows, table, (((1,), (1,)), ((), ())), preferred_element_type=F32)
    columns = offset + jnp.arange(shard_rows, dtype=jnp.int32)
    hit = local_target[:, None] == columns[None, :]
    local_pick = jnp.sum(jnp.where(hit, logits, F32(0.0)), axis=1)
    local_max = jnp.max(logits, axis=1)
    local_total = jnp.sum(jnp.exp(logits - local_max[:, None]), axis=1)
    mine = jnp.dot(jnp.stack([local_max, local_total, local_pick]), order, precision=EXACT)
    mine_all = jnp.broadcast_to(flipped(mine), (lax.axis_size(VOCAB), *mine.shape))
    everyone = lax.all_to_all(mine_all, VOCAB, 0, 0, tiled=True)

    ids = after(ids, mine_all)
    own_in, own_target = ids
    other_in, other_target = swap(ids, "za")

    weights = jnp.exp(logits - after(local_max, mine_all)[:, None]).astype(BF16)
    weights = jnp.dot(order.T.astype(BF16), weights, preferred_element_type=F32).astype(BF16)
    chips, quarter = ny * nx, half_rows // 4
    blocks = jnp.stack([2 * zb + c, 2 - 2 * zb + c, 2 * zb + 1 - c, 3 - 2 * zb - c])
    within = jnp.arange(half_rows, dtype=jnp.int32)
    wanted = blocks[within // quarter] * quarter + within % quarter
    choose = lambda side: (
        jnp.arange(shard_rows, dtype=jnp.int32)[:, None] == side * half_rows + wanted[None, :]
    ).astype(BF16)
    pick_columns = lambda array, side: jnp.dot(array, side, preferred_element_type=F32).astype(BF16)
    own_side, other_side = lax.optimization_barrier((choose(za), choose(1 - za)))
    for_other = pick_columns(weights, other_side)
    other_weights = swap(for_other, "za")
    weights, own_side = lax.optimization_barrier((weights, own_side, for_other))[:2]
    summed, target_rows = hidden_product(
        weights, (own_target[:, None] == columns[None, :]).astype(BF16), table
    )
    half_columns = offset + half + wanted
    picks = [(ids[:, None] == half_columns[None, :]).astype(BF16) for ids in (other_in, own_in)]
    picks = jnp.concatenate([part.reshape(chips, 2 * block, half_rows) for part in picks], axis=1)
    picks = picks.reshape(-1, half_rows)

    top = jnp.max(everyone[:, 0], axis=0)
    total = jnp.sum(everyone[:, 1] * jnp.exp(everyone[:, 0] - top), axis=0)
    lse = top + jnp.log(total)
    token_loss = lse - jnp.sum(everyone[:, 2], axis=0)
    lse = flipped(lse)
    scale = jnp.exp(mine[0] - lse)
    lse_local = jnp.dot(order, lse, precision=EXACT)

    partial = (summed * scale[:, None] - target_rows.astype(F32)).astype(BF16)
    other_scale = swap(after(scale, partial), "za")
    lse_local = after(lse_local, partial)
    partial = lax.all_to_all(partial, ("y", "x"), 0, 0, tiled=True)

    dlogits = (jnp.exp(logits - lse_local[:, None]) - hit.astype(F32)).astype(BF16)
    own_dlogits = pick_columns(dlogits, own_side)
    other_hit = (other_target[:, None] == half_columns[None, :]).astype(F32)
    other_dlogits = (other_weights.astype(F32) * other_scale[:, None] - other_hit).astype(BF16)
    pieces = []
    for at_column in range(0, width, width // CHUNKS):
        keep, send = table_product(
            own_dlogits, other_dlogits, picks, rows, more, at_column, width // CHUNKS
        )
        own_dlogits = after(own_dlogits, send)
        got = swap(send, "c")
        mine, theirs = (k + g.astype(F32) for k, g in zip(cut(keep, 2), cut(got, 2)))
        pieces.append((mine, theirs.astype(BF16)))

    partial = after(partial, pieces[-1][1])
    parts = jnp.sum(partial.reshape(chips, 2, block, width).astype(F32), axis=0)
    last = [swap(theirs, "zb") for _, theirs in pieces]
    near_part = swap(after(parts[1], *(theirs for _, theirs in pieces)), "h")
    near_part, *last = lax.optimization_barrier((near_part, *last))
    hidden_grad = (parts[0] + near_part).astype(BF16)
    table_grad = jnp.concatenate(
        [mine + got.astype(F32) for (mine, _), got in zip(pieces, last)], axis=1
    )
    return (table_grad, hidden_grad, token_loss)


def solution(mesh):
    finer = Mesh(mesh.devices.reshape(2, 2, 2, 4, 4, 2), DP + VOCAB)
    in_specs = (P(VOCAB, None), P(DP + VOCAB, None), P(DP + VOCAB, None), P(DP), P(DP))
    out_specs = (P(VOCAB + DP, None), P(DP + VOCAB, None), P(DP))
    return jax.shard_map(
        shards, mesh=finer, in_specs=in_specs, out_specs=out_specs, check_vma=False
    )
```

time: 189 us -> 184 us (0.974)
  Pallas kernels: 7 us -> 23.2 us
  waiting for transfers between devices: 61.8 us -> 49.9 us
  starting transfers between devices: 61.9 us -> 56.5 us
  other arithmetic: 16.4 us -> 21.7 us
  local copies, waits for them, and re-layouts: 11.2 us -> 5.95 us
  matrix products: 15.3 us -> 11.3 us
    ppermute x24 -> x12, starting transfers between devices: 35.9 us -> 17.2 us  [shift(): return lax.ppermute(array, axis, [(i, (i + by) % n) for i in range(n)])]
    ppermute x9 -> x10, waiting for transfers between devices: 13.9 us -> 32.4 us  [swap(): return lax.ppermute(array, axis, [(i, n - 1 - i) for i in range(n)])]
    ppermute x24 -> x12, waiting for transfers between devices: 35 us -> 17.5 us  [shift(): return lax.ppermute(array, axis, [(i, (i + by) % n) for i in range(n)])]
    pallas_call x2 -> x3, Pallas kernels: 7 us -> 23.2 us  [the longest x2 12.4 us: table_product(): pl.pallas_call(functools.partial(table_product_kernel, chips), grid=(colu...]
    all_to_all x1 -> x2, waiting for transfers between devices: 10.6 us -> 0.01 us  [the longest x1 0.01 us: shards(): partial = lax.all_to_all(partial, ('y', 'x'), 0, 0, tiled=True)]
    convert_element_type x7 -> x10, other arithmetic: 4.01 us -> 13.6 us  [the longest x1 4.99 us: shards(): partial = (summed * scale[:, None] - target_rows.astype(F32)).astype(BF16)]
    all_to_all x1 -> x2, starting transfers between devices: 7.58 us -> 13.8 us  [the longest x1 7.17 us: shards(): partial = lax.all_to_all(partial, ('y', 'x'), 0, 0, tiled=True)]
    dot_general x3 -> x4, matrix products: 9.01 us -> 4.27 us  [the longest x2 3.61 us: shards(): jnp.dot(array, side, preferred_element_type=F32).astype(BF16)]
  transfers between devices with their start and end apart: 36 -> 26, of which waited for: 18 -> 10; matrix products, arithmetic and copies ran while one was open for 19% -> 17% of each run, Pallas kernels for 4% -> 13%
where the time goes in v1:
time: 184 us; the launch traced here: 183 us
  starting transfers between devices  56.5 us (31%)
  waiting for transfers between devices  49.9 us (27%)
  Pallas kernels  23.2 us (13%)
  other arithmetic  21.7 us (12%)
  between operations  14.5 us (8%)
  matrix products  11.3 us (6%)
  local copies, waits for them, and re-layouts  5.95 us (3%)
    ppermute x10, waiting for transfers between devices, swap(): return lax.ppermute(array, axis, [(i, n - 1 - i) for i in range(n)])  32.4 us
    ppermute x10, starting transfers between devices, swap(): return lax.ppermute(array, axis, [(i, n - 1 - i) for i in range(n)])  22 us
    ppermute x12, waiting for transfers between devices, shift(): return lax.ppermute(array, axis, [(i, (i + by) % n) for i in range(n)])  17.5 us
    ppermute x12, starting transfers between devices, shift(): return lax.ppermute(array, axis, [(i, (i + by) % n) for i in range(n)])  17.2 us
    pallas_call x2, Pallas kernels, table_product(): pl.pallas_call(functools.partial(table_product_kernel, chips), grid=(colu...  12.4 us
    pallas_call x1, Pallas kernels, hidden_product(): pl.pallas_call(hidden_product_kernel, grid=(columns // tile,), in_specs=[...  10.8 us
    all_to_all x1, starting transfers between devices, shards(): partial = lax.all_to_all(partial, ('y', 'x'), 0, 0, tiled=True)  7.17 us
    all_to_all x1, starting transfers between devices, shards(): everyone = lax.all_to_all(mine_all, VOCAB, 0, 0, tiled=True)  6.63 us
  transfers between devices with their start and end apart: 26, of which 10 were waited for; matrix products, arithmetic and copies ran while one was open for 17% of the time, Pallas kernels for 13%

profile of v1, /device:TPU:2, one launch (start us, length us, event | category | flops | bytes accessed | tf_op | source)
XLA Modules:
  0.0 183.0 jit_solution(5119962075078901690)
XLA Ops:
  7.2 0.8 constant_dynamic-update-slice_fusion.1
  8.1 0.8 constant_dynamic-update-slice_fusion
  8.9 3.3 %collective-permute-start = (bf16[16,4096]{1,0:T(8,128)(2,1)S(1)}, bf16[16,4096]{1,0:T(8,128)(2,1)S(1)}, u32[]{:S(2)}, u32[]{:S(2)}) collective-permute-start(bf16[16,4096]{1,0:T(8,128)(2,1)S(1)} %constant_dynamic-update-slice_fusion), channel_id=1, source_target_pairs={{0,128},{128,0},{1,129},{129,1},{2,130},{130,2},{3,131},{131,3},{4... | collective-permute-start | bytes 393224 | tf_op jit(solution)/shard_map/ppermute | solution.py:30
  12.2 5.4 %collective-permute-start.1 = (bf16[16,4096]{1,0:T(8,128)(2,1)S(1)}, bf16[16,4096]{1,0:T(8,128)(2,1)S(1)}, u32[]{:S(2)}, u32[]{:S(2)}) collective-permute-start(bf16[16,4096]{1,0:T(8,128)(2,1)S(1)} %constant_dynamic-update-slice_fusion), channel_id=1, source_target_pairs={{0,1},{1,0},{2,3},{3,2},{4,5},{5,4},{6,7},{7,6},{8,9},{9,8},{10,11... | collective-permute-start | bytes 393224 | tf_op jit(solution)/shard_map/ppermute | solution.py:30
  18.1 2.4 %collective-permute-start.7 = (bf16[8,4096]{1,0:T(8,128)(2,1)}, bf16[8,4096]{1,0:T(8,128)(2,1)S(1)}, u32[]{:S(2)}, u32[]{:S(2)}) collective-permute-start(bf16[8,4096]{1,0:T(8,128)(2,1)} %param.6), channel_id=1, source_target_pairs={{0,4},{2,6},{4,0},{6,2},{1,5},{3,7},{5,1},{7,3},{8,12},{10,14},{12... | collective-permute-start | bytes 196616 | tf_op jit(solution)/shard_map/ppermute | solution.py:25
  20.5 1.8 collective-permute-start.6
  22.5 0.7 pad_add_fusion
  23.8 2.7 %collective-permute-done.1 = bf16[16,4096]{1,0:T(8,128)(2,1)S(1)} collective-permute-done((bf16[16,4096]{1,0:T(8,128)(2,1)S(1)}, bf16[16,4096]{1,0:T(8,128)(2,1)S(1)}, u32[]{:S(2)}, u32[]{:S(2)}) %collective-permute-start.1) | collective-permute-done | bytes 131104 | tf_op jit(solution)/shard_map/ppermute | solution.py:30
  26.4 3.5 %collective-permute-start.5 = (bf16[16,4096]{1,0:T(8,128)(2,1)S(1)}, bf16[16,4096]{1,0:T(8,128)(2,1)S(1)}, u32[]{:S(2)}, u32[]{:S(2)}) collective-permute-start(bf16[16,4096]{1,0:T(8,128)(2,1)S(1)} %constant_dynamic-update-slice_fusion), channel_id=1, source_target_pairs={{0,129},{129,0},{1,128},{128,1},{2,131},{131,2},{3,130},{130,3},{4... | collective-permute-start | bytes 393224 | tf_op jit(solution)/shard_map/ppermute | solution.py:145
  29.9 3.1 %collective-permute-start.4 = (bf16[8,4096]{1,0:T(8,128)(2,1)S(1)}, bf16[8,4096]{1,0:T(8,128)(2,1)S(1)}, u32[]{:S(2)}, u32[]{:S(2)}) collective-permute-start(bf16[8,4096]{1,0:T(8,128)(2,1)S(1)} %slice.91), channel_id=1, source_target_pairs={{0,24},{8,0},{16,8},{24,16},{1,25},{9,1},{17,9},{25,17},{2,26},{10... | collective-permute-start | bytes 196616 | tf_op jit(solution)/shard_map/ppermute | solution.py:25
  33.7 1.0 collective-permute-start.2
  34.6 0.9 pad_maximum_fusion.2
  35.5 3.6 %collective-permute-done.3 = bf16[8,4096]{1,0:T(8,128)(2,1)S(1)} collective-permute-done((bf16[8,4096]{1,0:T(8,128)(2,1)S(1)}, bf16[8,4096]{1,0:T(8,128)(2,1)S(1)}, u32[]{:S(2)}, u32[]{:S(2)}) %collective-permute-start.3) | collective-permute-done | bytes 65568 | tf_op jit(solution)/shard_map/ppermute | solution.py:25
  39.7 0.8 copy-done.4
  40.6 1.8 fusion
  42.4 3.1 %collective-permute-start.10 = (bf16[32,4096]{1,0:T(8,128)(2,1)S(1)}, bf16[32,4096]{1,0:T(8,128)(2,1)S(1)}, u32[]{:S(2)}, u32[]{:S(2)}) collective-permute-start(bf16[32,4096]{1,0:T(8,128)(2,1)S(1)} %pad_maximum_fusion.2), channel_id=1, source_target_pairs={{0,16},{8,24},{16,0},{24,8},{1,17},{9,25},{17,1},{25,9},{2,18},{10... | collective-permute-start | bytes 786440 | tf_op jit(solution)/shard_map/ppermute | solution.py:25
  45.5 1.5 collective-permute-start.11
  47.0 1.5 collective-permute-start.12
  48.5 1.1 collective-permute-start.13
  49.6 3.2 %collective-permute-done.9 = bf16[32,4096]{1,0:T(8,128)(2,1)S(1)} collective-permute-done((bf16[32,4096]{1,0:T(8,128)(2,1)S(1)}, bf16[32,4096]{1,0:T(8,128)(2,1)S(1)}, u32[]{:S(2)}, u32[]{:S(2)}) %collective-permute-start.9) | collective-permute-done | bytes 262176 | tf_op jit(solution)/shard_map/ppermute | solution.py:25
  53.4 3.7 %collective-permute-done.11 = bf16[32,4096]{1,0:T(8,128)(2,1)S(1)} collective-permute-done((bf16[32,4096]{1,0:T(8,128)(2,1)S(1)}, bf16[32,4096]{1,0:T(8,128)(2,1)S(1)}, u32[]{:S(2)}, u32[]{:S(2)}) %collective-permute-start.11) | collective-permute-done | bytes 262176 | tf_op jit(solution)/shard_map/ppermute | solution.py:25
  57.1 0.8 collective-permute-done.13
  58.0 5.8 %collective-permute-done.14 = bf16[32,4096]{1,0:T(8,128)(2,1)S(1)} collective-permute-done((bf16[32,4096]{1,0:T(8,128)(2,1)S(1)}, bf16[32,4096]{1,0:T(8,128)(2,1)S(1)}, u32[]{:S(2)}, u32[]{:S(2)}) %collective-permute-start.14) | collective-permute-done | bytes 262176 | tf_op jit(solution)/shard_map/ppermute | solution.py:25
  63.8 6.6 %fusion.43 = (f32[256]{0:T(256)S(1)}, f32[256,1024]{1,0:T(8,128)S(1)}) fusion(bf16[256,4096]{1,0:T(8,128)(2,1)S(1)} %constant_dynamic-update-slice_fusion.3.rows_ref, bf16[1024,4096]{1,0:T(8,128)(2,1)} %table_ref.1), kind=kOutput, calls=%fused_computation.133 | convolution fusion | flops 2147745536 | bytes 11535360 | tf_op jit(solution)/shard_map/dot_general | solution.py:158
  72.1 6.6 %all-to-all-start = ((f32[32,3,256]{2,1,0:T(4,128)}), f32[32,3,256]{2,1,0:T(4,128)S(1)}, u32[]{:S(2)}, u32[]{:S(2)}) async-start(f32[32,3,256]{2,1,0:T(4,128)} %broadcast_in_dim.7), calls=%async_computation | async-start | bytes 262144 | tf_op jit(solution)/shard_map/all_to_all | solution.py:166
  79.2 1.2 convolution_convert_fusion.2
  80.3 1.4 collective-permute-start.15
  81.7 1.6 collective-permute-start.17
  83.3 0.9 compare_convert_fusion.1.hit_ref
  84.2 10.8 %shard_map.76 = (f32[256,4096]{1,0:T(8,128)}, bf16[256,4096]{1,0:T(8,128)(2,1)}) custom-call(bf16[256,1024]{1,0:T(8,128)(2,1)} %copy-done.1, bf16[256,1024]{1,0:T(8,128)(2,1)} %compare_convert_fusion.1.hit_ref, bf16[1024,4096]{1,0:T(8,128)(2,1)} %table_ref.1), custom_call_target="tpu_custom_call" | custom-call | flops 4294967296 | bytes 15728640 | tf_op jit(solution)/shard_map/pallas_call | solution.py:47
  95.4 0.9 add_convert_fusion.2
  97.4 5.0 %subtract_convert_fusion = bf16[256,4096]{1,0:T(8,128)(2,1)} fusion(bf16[256,4096]{1,0:T(8,128)(2,1)} %get-tuple-element.42, f32[256,4096]{1,0:T(8,128)} %get-tuple-element.41, f32[256]{0:T(256)S(1)} %subtract_exponential_fusion), kind=kLoop, calls=%fused_computation.1 | loop fusion | flops 4194304 | bytes 8389632 | tf_op jit(solution)/shard_map/convert_element_type | solution.py:202
  102.4 7.2 %all-to-all-start.1 = ((bf16[16,16,4096]{2,1,0:T(8,128)(2,1)}), bf16[16,16,4096]{2,1,0:T(8,128)(2,1)S(1)}, u32[]{:S(2)}, u32[]{:S(2)}) async-start(bf16[16,16,4096]{2,1,0:T(8,128)(2,1)} %bitcast.13), calls=%async_computation.1 | async-start | bytes 4194304 | tf_op jit(solution)/shard_map/all_to_all | solution.py:205
  109.8 1.4 collective-permute-start.16
  111.3 2.5 %convolution_convert_fusion.1.own_ref = bf16[256,512]{1,0:T(8,128)(2,1)} fusion(bf16[1024,512]{1,0:T(8,128)(2,1)} %get-tuple-element.44, f32[256,1024]{1,0:T(8,128)S(1)} %get-tuple-element.75, f32[256]{0:T(256)S(1)} %bitcast.75, s32[1024]{0:T(1024)S(1)} %iota_add_fusion, s32[256]{0:T(256)S(1)} %convert_element_type.98), kind=kOutput, calls=%fused_computation.10 | convolution fusion | flops 269877248 | bytes 2365440 | tf_op jit(solution)/shard_map/dot_general | solution.py:181
  114.4 1.8 %subtract_convert_fusion.1.other_ref = bf16[256,512]{1,0:T(8,128)(2,1)} fusion(bf16[256,512]{1,0:T(8,128)(2,1)} %collective-permute-done.15, s32[512]{0:T(512)S(1)} %get-tuple-element.71, f32[256]{0:T(256)S(1)} %collective-permute-done.16, s32[256]{0:T(256)S(1)} %bitcast.71), kind=kLoop, calls=%fused_computation.23 | loop fusion | flops 786432 | bytes 528384 | tf_op jit(solution)/shard_map/convert_element_type | solution.py:210
  116.2 6.2 %shard_map.77 = (f32[256,2048]{1,0:T(8,128)}, bf16[256,2048]{1,0:T(8,128)(2,1)}) custom-call(bf16[256,512]{1,0:T(8,128)(2,1)} %convolution_convert_fusion.1.own_ref, bf16[256,512]{1,0:T(8,128)(2,1)} %subtract_convert_fusion.1.other_ref, bf16[512,512]{1,0:T(8,128)(2,1)} %bitcast.55, bf16[256,4096]{1,0:T(8,128)(2,1)} %copy-done, ...), custom_call_target="tpu_custom_call" | custom-call | flops 2147483648 | bytes 8388608 | tf_op jit(solution)/shard_map/pallas_call | solution.py:84
  122.4 6.2 %shard_map.78 = (f32[256,2048]{1,0:T(8,128)}, bf16[256,2048]{1,0:T(8,128)(2,1)}) custom-call(bf16[256,512]{1,0:T(8,128)(2,1)} %convolution_convert_fusion.1.own_ref, bf16[256,512]{1,0:T(8,128)(2,1)} %subtract_convert_fusion.1.other_ref, bf16[512,512]{1,0:T(8,128)(2,1)} %bitcast.56, bf16[256,4096]{1,0:T(8,128)(2,1)} %copy-done, ...), custom_call_target="tpu_custom_call" | custom-call | flops 2147483648 | bytes 8388608 | tf_op jit(solution)/shard_map/pallas_call | solution.py:84
  129.1 3.0 %collective-permute-done.19 = bf16[256,2048]{1,0:T(8,128)(2,1)S(1)} collective-permute-done((bf16[256,2048]{1,0:T(8,128)(2,1)}, bf16[256,2048]{1,0:T(8,128)(2,1)S(1)}, u32[]{:S(2)}, u32[]{:S(2)}) %collective-permute-start.19) | collective-permute-done | bytes 1048608 | tf_op jit(solution)/shard_map/ppermute | solution.py:30
  132.2 2.1 %add_convert_fusion.1 = bf16[128,2048]{1,0:T(8,128)(2,1)} fusion(f32[256,2048]{1,0:T(8,128)} %get-tuple-element.50, bf16[256,2048]{1,0:T(8,128)(2,1)S(1)} %collective-permute-done.19), kind=kLoop, calls=%fused_computation.18 | loop fusion | flops 786432 | bytes 2097152 | tf_op jit(solution)/shard_map/convert_element_type | solution.py:219
  134.3 2.9 %collective-permute-start.22 = (bf16[128,2048]{1,0:T(8,128)(2,1)}, bf16[128,2048]{1,0:T(8,128)(2,1)}, u32[]{:S(2)}, u32[]{:S(2)}) collective-permute-start(bf16[128,2048]{1,0:T(8,128)(2,1)} %add_convert_fusion.1), channel_id=1, source_target_pairs={{0,64},{64,0},{1,65},{65,1},{2,66},{66,2},{3,67},{67,3},{4,68},{68... | collective-permute-start | bytes 1572872 | tf_op jit(solution)/shard_map/ppermute | solution.py:30
  137.5 1.3 copy-done.2
  138.8 1.2 add_convert_fusion
  140.1 5.5 %collective-permute-start.20 = (f32[8,4096]{1,0:T(8,128)S(1)}, f32[8,4096]{1,0:T(8,128)S(1)}, u32[]{:S(2)}, u32[]{:S(2)}) collective-permute-start(f32[8,4096]{1,0:T(8,128)S(1)} %slice_bitcast_fusion.1), channel_id=1, source_target_pairs={{0,1},{1,0},{2,3},{3,2},{4,5},{5,4},{6,7},{7,6},{8,9},{9,8},{10,11... | collective-permute-start | bytes 393224 | tf_op jit(solution)/shard_map/ppermute | solution.py:30
  145.5 26.0 %collective-permute-done.20 = f32[8,4096]{1,0:T(8,128)S(1)} collective-permute-done((f32[8,4096]{1,0:T(8,128)S(1)}, f32[8,4096]{1,0:T(8,128)S(1)}, u32[]{:S(2)}, u32[]{:S(2)}) %collective-permute-start.20) | collective-permute-done | bytes 131104 | tf_op jit(solution)/shard_map/ppermute | solution.py:30
  172.2 1.2 convert_add_fusion
  173.5 1.2 convert_add_fusion.1
  174.7 1.5 pad_maximum_fusion
  (96 shorter events, 9.2 us)
Async XLA Ops:
  7.2 32.5 %copy-start.5 = (bf16[8,4096]{1,0:T(8,128)(2,1)S(1)}, bf16[8,4096]{1,0:T(8,128)(2,1)}, u32[]{:S(2)}) copy-start(bf16[8,4096]{1,0:T(8,128)(2,1)} %param.7) | copy-start | bytes 196612
  7.2 109.0 %all-gather.2.cloned.1.call-start = ((), (), s32[]{:S(2)}) async-start(), calls=%async_computation.2 | async-start | bytes 6684672 | tf_op jit(solution)/shard_map/all_gather | solution.py:154
  8.9 30.6 %collective-permute-start = (bf16[16,4096]{1,0:T(8,128)(2,1)S(1)}, bf16[16,4096]{1,0:T(8,128)(2,1)S(1)}, u32[]{:S(2)}, u32[]{:S(2)}) collective-permute-start(bf16[16,4096]{1,0:T(8,128)(2,1)S(1)} %constant_dynamic-update-slice_fusion), channel_id=1, source_target_pairs={{0,128},{128,0},{1,129},{129,1},{2,130},{130,2},{3,131},{131,3},{4... | collective-permute-start | bytes 393224 | tf_op jit(solution)/shard_map/ppermute | solution.py:30
  12.2 14.2 %collective-permute-start.1 = (bf16[16,4096]{1,0:T(8,128)(2,1)S(1)}, bf16[16,4096]{1,0:T(8,128)(2,1)S(1)}, u32[]{:S(2)}, u32[]{:S(2)}) collective-permute-start(bf16[16,4096]{1,0:T(8,128)(2,1)S(1)} %constant_dynamic-update-slice_fusion), channel_id=1, source_target_pairs={{0,1},{1,0},{2,3},{3,2},{4,5},{5,4},{6,7},{7,6},{8,9},{9,8},{10,11... | collective-permute-start | bytes 393224 | tf_op jit(solution)/shard_map/ppermute | solution.py:30
  17.6 12.4 %collective-permute-start.8 = (bf16[8,4096]{1,0:T(8,128)(2,1)}, bf16[8,4096]{1,0:T(8,128)(2,1)S(1)}, u32[]{:S(2)}, u32[]{:S(2)}) collective-permute-start(bf16[8,4096]{1,0:T(8,128)(2,1)} %param.6), channel_id=1, source_target_pairs={{0,6},{2,0},{4,2},{6,4},{1,7},{3,1},{5,3},{7,5},{8,14},{10,8},{12,... | collective-permute-start | bytes 196616 | tf_op jit(solution)/shard_map/ppermute | solution.py:25
  18.1 14.9 %collective-permute-start.7 = (bf16[8,4096]{1,0:T(8,128)(2,1)}, bf16[8,4096]{1,0:T(8,128)(2,1)S(1)}, u32[]{:S(2)}, u32[]{:S(2)}) collective-permute-start(bf16[8,4096]{1,0:T(8,128)(2,1)} %param.6), channel_id=1, source_target_pairs={{0,4},{2,6},{4,0},{6,2},{1,5},{3,7},{5,1},{7,3},{8,12},{10,14},{12... | collective-permute-start | bytes 196616 | tf_op jit(solution)/shard_map/ppermute | solution.py:25
  20.5 13.1 %collective-permute-start.6 = (bf16[8,4096]{1,0:T(8,128)(2,1)}, bf16[8,4096]{1,0:T(8,128)(2,1)S(1)}, u32[]{:S(2)}, u32[]{:S(2)}) collective-permute-start(bf16[8,4096]{1,0:T(8,128)(2,1)} %param.6), channel_id=1, source_target_pairs={{0,2},{2,4},{4,6},{6,0},{1,3},{3,5},{5,7},{7,1},{8,10},{10,12},{12... | collective-permute-start | bytes 196616 | tf_op jit(solution)/shard_map/ppermute | solution.py:25
  26.4 13.1 %collective-permute-start.5 = (bf16[16,4096]{1,0:T(8,128)(2,1)S(1)}, bf16[16,4096]{1,0:T(8,128)(2,1)S(1)}, u32[]{:S(2)}, u32[]{:S(2)}) collective-permute-start(bf16[16,4096]{1,0:T(8,128)(2,1)S(1)} %constant_dynamic-update-slice_fusion), channel_id=1, source_target_pairs={{0,129},{129,0},{1,128},{128,1},{2,131},{131,2},{3,130},{130,3},{4... | collective-permute-start | bytes 393224 | tf_op jit(solution)/shard_map/ppermute | solution.py:145
  29.9 5.6 %collective-permute-start.4 = (bf16[8,4096]{1,0:T(8,128)(2,1)S(1)}, bf16[8,4096]{1,0:T(8,128)(2,1)S(1)}, u32[]{:S(2)}, u32[]{:S(2)}) collective-permute-start(bf16[8,4096]{1,0:T(8,128)(2,1)S(1)} %slice.91), channel_id=1, source_target_pairs={{0,24},{8,0},{16,8},{24,16},{1,25},{9,1},{17,9},{25,17},{2,26},{10... | collective-permute-start | bytes 196616 | tf_op jit(solution)/shard_map/ppermute | solution.py:25
  33.0 6.1 %collective-permute-start.3 = (bf16[8,4096]{1,0:T(8,128)(2,1)S(1)}, bf16[8,4096]{1,0:T(8,128)(2,1)S(1)}, u32[]{:S(2)}, u32[]{:S(2)}) collective-permute-start(bf16[8,4096]{1,0:T(8,128)(2,1)S(1)} %slice.91), channel_id=1, source_target_pairs={{0,16},{8,24},{16,0},{24,8},{1,17},{9,25},{17,1},{25,9},{2,18},{10... | collective-permute-start | bytes 196616 | tf_op jit(solution)/shard_map/ppermute | solution.py:25
  33.7 5.8 %collective-permute-start.2 = (bf16[8,4096]{1,0:T(8,128)(2,1)S(1)}, bf16[8,4096]{1,0:T(8,128)(2,1)S(1)}, u32[]{:S(2)}, u32[]{:S(2)}) collective-permute-start(bf16[8,4096]{1,0:T(8,128)(2,1)S(1)} %slice.91), channel_id=1, source_target_pairs={{0,8},{8,16},{16,24},{24,0},{1,9},{9,17},{17,25},{25,1},{2,10},{10... | collective-permute-start | bytes 196616 | tf_op jit(solution)/shard_map/ppermute | solution.py:25
  39.7 0.8 copy-start.4
  42.4 10.4 %collective-permute-start.9 = (bf16[32,4096]{1,0:T(8,128)(2,1)S(1)}, bf16[32,4096]{1,0:T(8,128)(2,1)S(1)}, u32[]{:S(2)}, u32[]{:S(2)}) collective-permute-start(bf16[32,4096]{1,0:T(8,128)(2,1)S(1)} %pad_maximum_fusion.2), channel_id=1, source_target_pairs={{0,8},{8,16},{16,24},{24,0},{1,9},{9,17},{17,25},{25,1},{2,10},{10... | collective-permute-start | bytes 786440 | tf_op jit(solution)/shard_map/ppermute | solution.py:25
  42.4 10.9 %collective-permute-start.10 = (bf16[32,4096]{1,0:T(8,128)(2,1)S(1)}, bf16[32,4096]{1,0:T(8,128)(2,1)S(1)}, u32[]{:S(2)}, u32[]{:S(2)}) collective-permute-start(bf16[32,4096]{1,0:T(8,128)(2,1)S(1)} %pad_maximum_fusion.2), channel_id=1, source_target_pairs={{0,16},{8,24},{16,0},{24,8},{1,17},{9,25},{17,1},{25,9},{2,18},{10... | collective-permute-start | bytes 786440 | tf_op jit(solution)/shard_map/ppermute | solution.py:25
  45.5 11.6 %collective-permute-start.11 = (bf16[32,4096]{1,0:T(8,128)(2,1)S(1)}, bf16[32,4096]{1,0:T(8,128)(2,1)S(1)}, u32[]{:S(2)}, u32[]{:S(2)}) collective-permute-start(bf16[32,4096]{1,0:T(8,128)(2,1)S(1)} %pad_maximum_fusion.2), channel_id=1, source_target_pairs={{0,24},{8,0},{16,8},{24,16},{1,25},{9,1},{17,9},{25,17},{2,26},{10... | collective-permute-start | bytes 786440 | tf_op jit(solution)/shard_map/ppermute | solution.py:25
  47.0 10.1 %collective-permute-start.12 = (bf16[32,4096]{1,0:T(8,128)(2,1)S(1)}, bf16[32,4096]{1,0:T(8,128)(2,1)S(1)}, u32[]{:S(2)}, u32[]{:S(2)}) collective-permute-start(bf16[32,4096]{1,0:T(8,128)(2,1)S(1)} %pad_maximum_fusion.1), channel_id=1, source_target_pairs={{0,2},{2,4},{4,6},{6,0},{1,3},{3,5},{5,7},{7,1},{8,10},{10,12},{12... | collective-permute-start | bytes 786440 | tf_op jit(solution)/shard_map/ppermute | solution.py:25
  48.5 9.5 %collective-permute-start.13 = (bf16[32,4096]{1,0:T(8,128)(2,1)S(1)}, bf16[32,4096]{1,0:T(8,128)(2,1)S(1)}, u32[]{:S(2)}, u32[]{:S(2)}) collective-permute-start(bf16[32,4096]{1,0:T(8,128)(2,1)S(1)} %pad_maximum_fusion.1), channel_id=1, source_target_pairs={{0,4},{2,6},{4,0},{6,2},{1,5},{3,7},{5,1},{7,3},{8,12},{10,14},{12... | collective-permute-start | bytes 786440 | tf_op jit(solution)/shard_map/ppermute | solution.py:25
  52.8 11.0 %collective-permute-start.14 = (bf16[32,4096]{1,0:T(8,128)(2,1)S(1)}, bf16[32,4096]{1,0:T(8,128)(2,1)S(1)}, u32[]{:S(2)}, u32[]{:S(2)}) collective-permute-start(bf16[32,4096]{1,0:T(8,128)(2,1)S(1)} %pad_maximum_fusion.1), channel_id=1, source_target_pairs={{0,6},{2,0},{4,2},{6,4},{1,7},{3,1},{5,3},{7,5},{8,14},{10,8},{12,... | collective-permute-start | bytes 786440 | tf_op jit(solution)/shard_map/ppermute | solution.py:25
  63.8 6.6 %copy-start = (bf16[256,4096]{1,0:T(8,128)(2,1)}, bf16[256,4096]{1,0:T(8,128)(2,1)S(1)}, u32[]{:S(2)}) copy-start(bf16[256,4096]{1,0:T(8,128)(2,1)S(1)} %constant_dynamic-update-slice_fusion.3.rows_ref) | copy-start | bytes 6291460
  71.0 9.3 %copy-start.6 = (f32[3,256]{1,0:T(4,128)}, f32[3,256]{1,0:T(4,128)S(1)}, u32[]{:S(2)}) copy-start(f32[3,256]{1,0:T(4,128)S(1)} %fusion.20) | copy-start | bytes 9220
  72.1 24.2 %all-to-all-start = ((f32[32,3,256]{2,1,0:T(4,128)}), f32[32,3,256]{2,1,0:T(4,128)S(1)}, u32[]{:S(2)}, u32[]{:S(2)}) async-start(f32[32,3,256]{2,1,0:T(4,128)} %broadcast_in_dim.7), calls=%async_computation | async-start | bytes 262144 | tf_op jit(solution)/shard_map/all_to_all | solution.py:166
  79.2 5.1 %copy-start.1 = (bf16[256,1024]{1,0:T(8,128)(2,1)}, bf16[256,1024]{1,0:T(8,128)(2,1)S(1)}, u32[]{:S(2)}) copy-start(bf16[256,1024]{1,0:T(8,128)(2,1)S(1)} %convolution_convert_fusion.weights_ref) | copy-start | bytes 1572868
  80.3 34.0 %collective-permute-start.15 = (bf16[256,512]{1,0:T(8,128)(2,1)}, bf16[256,512]{1,0:T(8,128)(2,1)}, u32[]{:S(2)}, u32[]{:S(2)}) collective-permute-start(bf16[256,512]{1,0:T(8,128)(2,1)} %convolution_convert_fusion.2), channel_id=1, source_target_pairs={{0,128},{128,0},{1,129},{129,1},{2,130},{130,2},{3,131},{131,3},{4... | collective-permute-start | bytes 786440 | tf_op jit(solution)/shard_map/ppermute | solution.py:30
  81.7 13.4 %collective-permute-start.17 = (s32[2,256]{1,0:T(2,128)S(1)}, s32[2,256]{1,0:T(2,128)S(1)}, u32[]{:S(2)}, u32[]{:S(2)}) collective-permute-start(s32[2,256]{1,0:T(2,128)S(1)} %reshape.249), channel_id=1, source_target_pairs={{0,128},{128,0},{1,129},{129,1},{2,130},{130,2},{3,131},{131,3},{4... | collective-permute-start | bytes 6152 | tf_op jit(solution)/shard_map/ppermute | solution.py:30
  84.2 13.2 %slice-start = ((f32[3,256]{1,0:T(4,128)}), f32[1,256]{1,0:T(1,128)S(1)}, s32[]{:S(2)}) async-start(f32[3,256]{1,0:T(4,128)} %copy-done.6), calls=%async_computation.3 | async-start | bytes 2048 | tf_op jit(solution)/shard_map/slice | solution.py:199
  102.4 34.8 %all-to-all-start.1 = ((bf16[16,16,4096]{2,1,0:T(8,128)(2,1)}), bf16[16,16,4096]{2,1,0:T(8,128)(2,1)S(1)}, u32[]{:S(2)}, u32[]{:S(2)}) async-start(bf16[16,16,4096]{2,1,0:T(8,128)(2,1)} %bitcast.13), calls=%async_computation.1 | async-start | bytes 4194304 | tf_op jit(solution)/shard_map/all_to_all | solution.py:205
  109.8 4.5 %collective-permute-start.16 = (f32[256]{0:T(256)S(1)}, f32[256]{0:T(256)S(1)}, u32[]{:S(2)}, u32[]{:S(2)}) collective-permute-start(f32[256]{0:T(256)S(1)} %subtract_exponential_fusion), channel_id=1, source_target_pairs={{0,128},{128,0},{1,129},{129,1},{2,130},{130,2},{3,131},{131,3},{4... | collective-permute-start | bytes 3080 | tf_op jit(solution)/shard_map/ppermute | solution.py:30
  128.6 3.5 %collective-permute-start.19 = (bf16[256,2048]{1,0:T(8,128)(2,1)}, bf16[256,2048]{1,0:T(8,128)(2,1)S(1)}, u32[]{:S(2)}, u32[]{:S(2)}) collective-permute-start(bf16[256,2048]{1,0:T(8,128)(2,1)} %get-tuple-element.51), channel_id=1, source_target_pairs={{0,32},{32,0},{1,33},{33,1},{2,34},{34,2},{3,35},{35,3},{4,36},{36... | collective-permute-start | bytes 3145736 | tf_op jit(solution)/shard_map/ppermute | solution.py:30
  128.6 8.8 %collective-permute-start.18 = (bf16[256,2048]{1,0:T(8,128)(2,1)}, bf16[256,2048]{1,0:T(8,128)(2,1)}, u32[]{:S(2)}, u32[]{:S(2)}) collective-permute-start(bf16[256,2048]{1,0:T(8,128)(2,1)} %get-tuple-element.48), channel_id=1, source_target_pairs={{0,32},{32,0},{1,33},{33,1},{2,34},{34,2},{3,35},{35,3},{4,36},{36... | collective-permute-start | bytes 3145736 | tf_op jit(solution)/shard_map/ppermute | solution.py:30
  134.3 37.3 %collective-permute-start.22 = (bf16[128,2048]{1,0:T(8,128)(2,1)}, bf16[128,2048]{1,0:T(8,128)(2,1)}, u32[]{:S(2)}, u32[]{:S(2)}) collective-permute-start(bf16[128,2048]{1,0:T(8,128)(2,1)} %add_convert_fusion.1), channel_id=1, source_target_pairs={{0,64},{64,0},{1,65},{65,1},{2,66},{66,2},{3,67},{67,3},{4,68},{68... | collective-permute-start | bytes 1572872 | tf_op jit(solution)/shard_map/ppermute | solution.py:30
  137.2 1.6 copy-start.2
  137.2 35.0 %copy-start.3 = (f32[256,2048]{1,0:T(8,128)S(1)}, f32[256,2048]{1,0:T(8,128)}, u32[]{:S(2)}) copy-start(f32[256,2048]{1,0:T(8,128)} %get-tuple-element.50) | copy-start | bytes 6291460
  139.9 31.6 %collective-permute-start.21 = (bf16[128,2048]{1,0:T(8,128)(2,1)S(1)}, bf16[128,2048]{1,0:T(8,128)(2,1)S(1)}, u32[]{:S(2)}, u32[]{:S(2)}) collective-permute-start(bf16[128,2048]{1,0:T(8,128)(2,1)S(1)} %add_convert_fusion), channel_id=1, source_target_pairs={{0,64},{64,0},{1,65},{65,1},{2,66},{66,2},{3,67},{67,3},{4,68},{68... | collective-permute-start | bytes 1572872 | tf_op jit(solution)/shard_map/ppermute | solution.py:30
  140.1 31.5 %collective-permute-start.20 = (f32[8,4096]{1,0:T(8,128)S(1)}, f32[8,4096]{1,0:T(8,128)S(1)}, u32[]{:S(2)}, u32[]{:S(2)}) collective-permute-start(f32[8,4096]{1,0:T(8,128)S(1)} %slice_bitcast_fusion.1), channel_id=1, source_target_pairs={{0,1},{1,0},{2,3},{3,2},{4,5},{5,4},{6,7},{7,6},{8,9},{9,8},{10,11... | collective-permute-start | bytes 393224 | tf_op jit(solution)/shard_map/ppermute | solution.py:30
Sparse Core Ops, SparseCore 0:
  40.6 63.1 all-gather.1

commit v2 on v1

--- a/solution.py
+++ b/solution.py
@@ -216,17 +216,13 @@
         own_dlogits = after(own_dlogits, send)
         got = swap(send, "c")
         mine, theirs = (k + g.astype(F32) for k, g in zip(cut(keep, 2), cut(got, 2)))
-        pieces.append((mine, theirs.astype(BF16)))
-
-    partial = after(partial, pieces[-1][1])
+        theirs = theirs.astype(BF16)
+        pieces.append((mine, swap(theirs, "zb")))
+    table_grad = jnp.concatenate([mine + last.astype(F32) for mine, last in pieces], axis=1)
+
+    partial = after(partial, theirs)
     parts = jnp.sum(partial.reshape(chips, 2, block, width).astype(F32), axis=0)
-    last = [swap(theirs, "zb") for _, theirs in pieces]
-    near_part = swap(after(parts[1], *(theirs for _, theirs in pieces)), "h")
-    near_part, *last = lax.optimization_barrier((near_part, *last))
-    hidden_grad = (parts[0] + near_part).astype(BF16)
-    table_grad = jnp.concatenate(
-        [mine + got.astype(F32) for (mine, _), got in zip(pieces, last)], axis=1
-    )
+    hidden_grad = (parts[0] + swap(parts[1], "h")).astype(BF16)
     return (table_grad, hidden_grad, token_loss)
 
 

time: 184 us -> 175 us (0.951); the launches traced: 183 us -> 172 us
  waiting for transfers between devices: 49.9 us -> 37.9 us
  starting transfers between devices: 56.5 us -> 58.7 us
    ppermute x10, waiting for transfers between devices: 32.4 us -> 24.3 us  [swap(): return lax.ppermute(array, axis, [(i, n - 1 - i) for i in range(n)])]
    all_to_all x1, starting transfers between devices: 6.63 us -> 12.4 us  [shards(): everyone = lax.all_to_all(mine_all, VOCAB, 0, 0, tiled=True)]
    ppermute x12, waiting for transfers between devices: 17.5 us -> 13.5 us  [shift(): return lax.ppermute(array, axis, [(i, (i + by) % n) for i in range(n)])]
    ppermute x1, starting transfers between devices: 3.51 us -> 0.01 us  [shards(): lax.ppermute(both, ('za', 'h'), [(0, 3), (3, 0), (1, 2), (2, 1)])]
  transfers between devices with their start and end apart: 26 -> 26, of which waited for: 10 -> 11; matrix products, arithmetic and copies ran while one was open for 17% -> 19% of each run, Pallas kernels for 13% -> 13%
where the time goes in v2:
time: 175 us; the launch traced here: 172 us
  starting transfers between devices  58.7 us (34%)
  waiting for transfers between devices  37.9 us (22%)
  Pallas kernels  23.2 us (13%)
  other arithmetic  21.8 us (12%)
  between operations  14.5 us (8%)
  matrix products  11.4 us (7%)
  local copies, waits for them, and re-layouts  4.64 us (3%)
    ppermute x10, waiting for transfers between devices, swap(): return lax.ppermute(array, axis, [(i, n - 1 - i) for i in range(n)])  24.3 us
    ppermute x10, starting transfers between devices, swap(): return lax.ppermute(array, axis, [(i, n - 1 - i) for i in range(n)])  20.9 us
    ppermute x12, starting transfers between devices, shift(): return lax.ppermute(array, axis, [(i, (i + by) % n) for i in range(n)])  18.1 us
    ppermute x12, waiting for transfers between devices, shift(): return lax.ppermute(array, axis, [(i, (i + by) % n) for i in range(n)])  13.5 us
    all_to_all x1, starting transfers between devices, shards(): everyone = lax.all_to_all(mine_all, VOCAB, 0, 0, tiled=True)  12.4 us
    pallas_call x2, Pallas kernels, table_product(): pl.pallas_call(functools.partial(table_product_kernel, chips), grid=(colu...  12.4 us
    pallas_call x1, Pallas kernels, hidden_product(): pl.pallas_call(hidden_product_kernel, grid=(columns // tile,), in_specs=[...  10.8 us
    all_to_all x1, starting transfers between devices, shards(): partial = lax.all_to_all(partial, ('y', 'x'), 0, 0, tiled=True)  7.16 us
  transfers between devices with their start and end apart: 26, of which 11 were waited for; matrix products, arithmetic and copies ran while one was open for 19% of the time, Pallas kernels for 13%

profile of v2, /device:TPU:2, one launch (start us, length us, event | category | flops | bytes accessed | tf_op | source)
XLA Modules:
  0.0 172.0 jit_solution(14881679992551350257)
XLA Ops:
  7.2 0.8 constant_dynamic-update-slice_fusion.1
  8.1 0.8 constant_dynamic-update-slice_fusion
  8.9 7.2 %collective-permute-start.1 = (bf16[16,4096]{1,0:T(8,128)(2,1)S(1)}, bf16[16,4096]{1,0:T(8,128)(2,1)S(1)}, u32[]{:S(2)}, u32[]{:S(2)}) collective-permute-start(bf16[16,4096]{1,0:T(8,128)(2,1)S(1)} %constant_dynamic-update-slice_fusion), channel_id=1, source_target_pairs={{0,1},{1,0},{2,3},{3,2},{4,5},{5,4},{6,7},{7,6},{8,9},{9,8},{10,11... | collective-permute-start | bytes 393224 | tf_op jit(solution)/shard_map/ppermute | solution.py:30
  16.1 1.5 collective-permute-start.6
  17.6 1.1 collective-permute-start.7
  18.7 2.2 %collective-permute-start.8 = (bf16[8,4096]{1,0:T(8,128)(2,1)}, bf16[8,4096]{1,0:T(8,128)(2,1)S(1)}, u32[]{:S(2)}, u32[]{:S(2)}) collective-permute-start(bf16[8,4096]{1,0:T(8,128)(2,1)} %param.6), channel_id=1, source_target_pairs={{0,6},{2,0},{4,2},{6,4},{1,7},{3,1},{5,3},{7,5},{8,14},{10,8},{12,... | collective-permute-start | bytes 196616 | tf_op jit(solution)/shard_map/ppermute | solution.py:25
  20.9 0.7 pad_add_fusion
  22.4 2.6 %collective-permute-start = (bf16[16,4096]{1,0:T(8,128)(2,1)S(1)}, bf16[16,4096]{1,0:T(8,128)(2,1)S(1)}, u32[]{:S(2)}, u32[]{:S(2)}) collective-permute-start(bf16[16,4096]{1,0:T(8,128)(2,1)S(1)} %constant_dynamic-update-slice_fusion), channel_id=1, source_target_pairs={{0,128},{128,0},{1,129},{129,1},{2,130},{130,2},{3,131},{131,3},{4... | collective-permute-start | bytes 393224 | tf_op jit(solution)/shard_map/ppermute | solution.py:30
  25.0 1.7 collective-permute-start.2
  26.6 2.9 %collective-permute-start.3 = (bf16[8,4096]{1,0:T(8,128)(2,1)S(1)}, bf16[8,4096]{1,0:T(8,128)(2,1)S(1)}, u32[]{:S(2)}, u32[]{:S(2)}) collective-permute-start(bf16[8,4096]{1,0:T(8,128)(2,1)S(1)} %slice.91), channel_id=1, source_target_pairs={{0,16},{8,24},{16,0},{24,8},{1,17},{9,25},{17,1},{25,9},{2,18},{10... | collective-permute-start | bytes 196616 | tf_op jit(solution)/shard_map/ppermute | solution.py:25
  29.6 1.3 collective-permute-start.4
  30.9 0.9 pad_maximum_fusion.2
  31.8 0.7 collective-permute-done.3
  32.5 1.3 collective-permute-done.4
  34.0 0.8 copy-done.4
  34.9 1.8 %fusion = (bf16[1024,512]{1,0:T(8,128)(2,1)}, bf16[1024,512]{1,0:T(8,128)(2,1)S(1)}) fusion(s32[512]{0:T(512)S(1)} %get-tuple-element.65, s32[512]{0:T(512)S(1)} %get-tuple-element.64), kind=kLoop, calls=%fused_computation.5 | loop fusion | flops 2097152 | bytes 2101248 | tf_op jit(solution)/shard_map/convert_element_type | solution.py:180
  37.0 3.7 %collective-permute-start.10 = (bf16[32,4096]{1,0:T(8,128)(2,1)S(1)}, bf16[32,4096]{1,0:T(8,128)(2,1)S(1)}, u32[]{:S(2)}, u32[]{:S(2)}) collective-permute-start(bf16[32,4096]{1,0:T(8,128)(2,1)S(1)} %pad_maximum_fusion.2), channel_id=1, source_target_pairs={{0,16},{8,24},{16,0},{24,8},{1,17},{9,25},{17,1},{25,9},{2,18},{10... | collective-permute-start | bytes 786440 | tf_op jit(solution)/shard_map/ppermute | solution.py:25
  40.8 2.0 %collective-permute-start.12 = (bf16[32,4096]{1,0:T(8,128)(2,1)S(1)}, bf16[32,4096]{1,0:T(8,128)(2,1)S(1)}, u32[]{:S(2)}, u32[]{:S(2)}) collective-permute-start(bf16[32,4096]{1,0:T(8,128)(2,1)S(1)} %pad_maximum_fusion.1), channel_id=1, source_target_pairs={{0,2},{2,4},{4,6},{6,0},{1,3},{3,5},{5,7},{7,1},{8,10},{10,12},{12... | collective-permute-start | bytes 786440 | tf_op jit(solution)/shard_map/ppermute | solution.py:25
  43.4 2.8 %collective-permute-done.9 = bf16[32,4096]{1,0:T(8,128)(2,1)S(1)} collective-permute-done((bf16[32,4096]{1,0:T(8,128)(2,1)S(1)}, bf16[32,4096]{1,0:T(8,128)(2,1)S(1)}, u32[]{:S(2)}, u32[]{:S(2)}) %collective-permute-start.9) | collective-permute-done | bytes 262176 | tf_op jit(solution)/shard_map/ppermute | solution.py:25
  46.2 0.7 collective-permute-start.14
  47.0 2.1 %collective-permute-done.10 = bf16[32,4096]{1,0:T(8,128)(2,1)S(1)} collective-permute-done((bf16[32,4096]{1,0:T(8,128)(2,1)S(1)}, bf16[32,4096]{1,0:T(8,128)(2,1)S(1)}, u32[]{:S(2)}, u32[]{:S(2)}) %collective-permute-start.10) | collective-permute-done | bytes 262176 | tf_op jit(solution)/shard_map/ppermute | solution.py:25
  49.3 1.6 collective-permute-done.13
  51.0 4.8 %collective-permute-done.14 = bf16[32,4096]{1,0:T(8,128)(2,1)S(1)} collective-permute-done((bf16[32,4096]{1,0:T(8,128)(2,1)S(1)}, bf16[32,4096]{1,0:T(8,128)(2,1)S(1)}, u32[]{:S(2)}, u32[]{:S(2)}) %collective-permute-start.14) | collective-permute-done | bytes 262176 | tf_op jit(solution)/shard_map/ppermute | solution.py:25
  55.8 6.6 %fusion.43 = (f32[256]{0:T(256)S(1)}, f32[256,1024]{1,0:T(8,128)S(1)}) fusion(bf16[256,4096]{1,0:T(8,128)(2,1)S(1)} %constant_dynamic-update-slice_fusion.3.rows_ref, bf16[1024,4096]{1,0:T(8,128)(2,1)} %table_ref.1), kind=kOutput, calls=%fused_computation.133 | convolution fusion | flops 2147745536 | bytes 11535360 | tf_op jit(solution)/shard_map/dot_general | solution.py:158
  63.5 0.7 broadcast_in_dim.7
  64.1 12.4 %all-to-all-start = ((f32[32,3,256]{2,1,0:T(4,128)}), f32[32,3,256]{2,1,0:T(4,128)S(1)}, u32[]{:S(2)}, u32[]{:S(2)}) async-start(f32[32,3,256]{2,1,0:T(4,128)} %broadcast_in_dim.7), calls=%async_computation | async-start | bytes 262144 | tf_op jit(solution)/shard_map/all_to_all | solution.py:166
  77.1 1.2 convolution_convert_fusion.2
  78.3 2.9 %collective-permute-start.15 = (bf16[256,512]{1,0:T(8,128)(2,1)}, bf16[256,512]{1,0:T(8,128)(2,1)}, u32[]{:S(2)}, u32[]{:S(2)}) collective-permute-start(bf16[256,512]{1,0:T(8,128)(2,1)} %convolution_convert_fusion.2), channel_id=1, source_target_pairs={{0,128},{128,0},{1,129},{129,1},{2,130},{130,2},{3,131},{131,3},{4... | collective-permute-start | bytes 786440 | tf_op jit(solution)/shard_map/ppermute | solution.py:30
  81.2 0.9 compare_convert_fusion.1.hit_ref
  82.1 10.8 %shard_map.76 = (f32[256,4096]{1,0:T(8,128)}, bf16[256,4096]{1,0:T(8,128)(2,1)}) custom-call(bf16[256,1024]{1,0:T(8,128)(2,1)} %copy-done.1, bf16[256,1024]{1,0:T(8,128)(2,1)} %compare_convert_fusion.1.hit_ref, bf16[1024,4096]{1,0:T(8,128)(2,1)} %table_ref.1), custom_call_target="tpu_custom_call" | custom-call | flops 4294967296 | bytes 15728640 | tf_op jit(solution)/shard_map/pallas_call | solution.py:47
  93.3 0.9 add_convert_fusion.2
  95.3 5.1 %subtract_convert_fusion = bf16[256,4096]{1,0:T(8,128)(2,1)} fusion(bf16[256,4096]{1,0:T(8,128)(2,1)} %get-tuple-element.38, f32[256,4096]{1,0:T(8,128)} %get-tuple-element.37, f32[256]{0:T(256)S(1)} %subtract_exponential_fusion), kind=kLoop, calls=%fused_computation.1 | loop fusion | flops 4194304 | bytes 8389632 | tf_op jit(solution)/shard_map/convert_element_type | solution.py:202
  100.7 7.2 %all-to-all-start.1 = ((bf16[16,16,4096]{2,1,0:T(8,128)(2,1)}), bf16[16,16,4096]{2,1,0:T(8,128)(2,1)S(1)}, u32[]{:S(2)}, u32[]{:S(2)}) async-start(bf16[16,16,4096]{2,1,0:T(8,128)(2,1)} %bitcast.13), calls=%async_computation.1 | async-start | bytes 4194304 | tf_op jit(solution)/shard_map/all_to_all | solution.py:205
  107.9 2.5 %convolution_convert_fusion.1.own_ref = bf16[256,512]{1,0:T(8,128)(2,1)} fusion(bf16[1024,512]{1,0:T(8,128)(2,1)} %get-tuple-element.40, f32[256,1024]{1,0:T(8,128)S(1)} %get-tuple-element.67, f32[256]{0:T(256)S(1)} %bitcast.75, s32[1024]{0:T(1024)S(1)} %iota_add_fusion, s32[256]{0:T(256)S(1)} %convert_element_type.98), kind=kOutput, calls=%fused_computation.10 | convolution fusion | flops 269877248 | bytes 2365440 | tf_op jit(solution)/shard_map/dot_general | solution.py:181
  110.3 1.8 %subtract_convert_fusion.1.other_ref = bf16[256,512]{1,0:T(8,128)(2,1)} fusion(bf16[256,512]{1,0:T(8,128)(2,1)} %collective-permute-done.15, s32[512]{0:T(512)S(1)} %get-tuple-element.63, f32[256]{0:T(256)S(1)} %collective-permute-done.16, s32[256]{0:T(256)S(1)} %bitcast.71), kind=kLoop, calls=%fused_computation.23 | loop fusion | flops 786432 | bytes 528384 | tf_op jit(solution)/shard_map/convert_element_type | solution.py:210
  112.2 6.2 %shard_map.77 = (f32[256,2048]{1,0:T(8,128)}, bf16[256,2048]{1,0:T(8,128)(2,1)}) custom-call(bf16[256,512]{1,0:T(8,128)(2,1)} %convolution_convert_fusion.1.own_ref, bf16[256,512]{1,0:T(8,128)(2,1)} %subtract_convert_fusion.1.other_ref, bf16[512,512]{1,0:T(8,128)(2,1)} %bitcast.55, bf16[256,4096]{1,0:T(8,128)(2,1)} %copy-done, ...), custom_call_target="tpu_custom_call" | custom-call | flops 2147483648 | bytes 8388608 | tf_op jit(solution)/shard_map/pallas_call | solution.py:84
  118.4 6.2 %shard_map.78 = (f32[256,2048]{1,0:T(8,128)}, bf16[256,2048]{1,0:T(8,128)(2,1)}) custom-call(bf16[256,512]{1,0:T(8,128)(2,1)} %convolution_convert_fusion.1.own_ref, bf16[256,512]{1,0:T(8,128)(2,1)} %subtract_convert_fusion.1.other_ref, bf16[512,512]{1,0:T(8,128)(2,1)} %bitcast.56, bf16[256,4096]{1,0:T(8,128)(2,1)} %copy-done, ...), custom_call_target="tpu_custom_call" | custom-call | flops 2147483648 | bytes 8388608 | tf_op jit(solution)/shard_map/pallas_call | solution.py:84
  125.1 3.0 %collective-permute-done.20 = bf16[256,2048]{1,0:T(8,128)(2,1)S(1)} collective-permute-done((bf16[256,2048]{1,0:T(8,128)(2,1)}, bf16[256,2048]{1,0:T(8,128)(2,1)S(1)}, u32[]{:S(2)}, u32[]{:S(2)}) %collective-permute-start.20) | collective-permute-done | bytes 1048608 | tf_op jit(solution)/shard_map/ppermute | solution.py:30
  128.1 2.1 %add_convert_fusion = bf16[128,2048]{1,0:T(8,128)(2,1)} fusion(f32[256,2048]{1,0:T(8,128)} %get-tuple-element.46, bf16[256,2048]{1,0:T(8,128)(2,1)S(1)} %collective-permute-done.20), kind=kLoop, calls=%fused_computation.16 | loop fusion | flops 786432 | bytes 2097152 | tf_op jit(solution)/shard_map/convert_element_type | solution.py:219
  130.2 1.0 collective-permute-start.21
  131.5 5.4 %collective-permute-start.22 = (f32[8,4096]{1,0:T(8,128)S(1)}, f32[8,4096]{1,0:T(8,128)S(1)}, u32[]{:S(2)}, u32[]{:S(2)}) collective-permute-start(f32[8,4096]{1,0:T(8,128)S(1)} %slice_bitcast_fusion), channel_id=1, source_target_pairs={{0,1},{1,0},{2,3},{3,2},{4,5},{5,4},{6,7},{7,6},{8,9},{9,8},{10,11... | collective-permute-start | bytes 393224 | tf_op jit(solution)/shard_map/ppermute | solution.py:30
  136.9 1.2 add_convert_fusion.1
  138.1 1.2 collective-permute-start.19
  139.3 15.7 %collective-permute-done.22 = f32[8,4096]{1,0:T(8,128)S(1)} collective-permute-done((f32[8,4096]{1,0:T(8,128)S(1)}, f32[8,4096]{1,0:T(8,128)S(1)}, u32[]{:S(2)}, u32[]{:S(2)}) %collective-permute-start.22) | collective-permute-done | bytes 131104 | tf_op jit(solution)/shard_map/ppermute | solution.py:30
  155.7 5.5 %collective-permute-done.19 = bf16[128,2048]{1,0:T(8,128)(2,1)S(1)} collective-permute-done((bf16[128,2048]{1,0:T(8,128)(2,1)S(1)}, bf16[128,2048]{1,0:T(8,128)(2,1)S(1)}, u32[]{:S(2)}, u32[]{:S(2)}) %collective-permute-start.19) | collective-permute-done | bytes 524320 | tf_op jit(solution)/shard_map/ppermute | solution.py:30
  161.2 1.2 convert_add_fusion.1
  162.5 1.2 convert_add_fusion
  163.7 1.5 pad_maximum_fusion
  (96 shorter events, 7.1 us)
Async XLA Ops:
  7.2 26.8 %copy-start.5 = (bf16[8,4096]{1,0:T(8,128)(2,1)S(1)}, bf16[8,4096]{1,0:T(8,128)(2,1)}, u32[]{:S(2)}) copy-start(bf16[8,4096]{1,0:T(8,128)(2,1)} %param.7) | copy-start | bytes 196612
  7.2 105.0 %all-gather.2.cloned.1.call-start = ((), (), s32[]{:S(2)}) async-start(), calls=%async_computation.2 | async-start | bytes 6684672 | tf_op jit(solution)/shard_map/all_gather | solution.py:154
  8.9 13.4 %collective-permute-start.1 = (bf16[16,4096]{1,0:T(8,128)(2,1)S(1)}, bf16[16,4096]{1,0:T(8,128)(2,1)S(1)}, u32[]{:S(2)}, u32[]{:S(2)}) collective-permute-start(bf16[16,4096]{1,0:T(8,128)(2,1)S(1)} %constant_dynamic-update-slice_fusion), channel_id=1, source_target_pairs={{0,1},{1,0},{2,3},{3,2},{4,5},{5,4},{6,7},{7,6},{8,9},{9,8},{10,11... | collective-permute-start | bytes 393224 | tf_op jit(solution)/shard_map/ppermute | solution.py:30
  16.1 17.7 %collective-permute-start.5 = (bf16[16,4096]{1,0:T(8,128)(2,1)S(1)}, bf16[16,4096]{1,0:T(8,128)(2,1)S(1)}, u32[]{:S(2)}, u32[]{:S(2)}) collective-permute-start(bf16[16,4096]{1,0:T(8,128)(2,1)S(1)} %constant_dynamic-update-slice_fusion), channel_id=1, source_target_pairs={{0,129},{129,0},{1,128},{128,1},{2,131},{131,2},{3,130},{130,3},{4... | collective-permute-start | bytes 393224 | tf_op jit(solution)/shard_map/ppermute | solution.py:145
  16.1 8.9 %collective-permute-start.6 = (bf16[8,4096]{1,0:T(8,128)(2,1)}, bf16[8,4096]{1,0:T(8,128)(2,1)S(1)}, u32[]{:S(2)}, u32[]{:S(2)}) collective-permute-start(bf16[8,4096]{1,0:T(8,128)(2,1)} %param.6), channel_id=1, source_target_pairs={{0,2},{2,4},{4,6},{6,0},{1,3},{3,5},{5,7},{7,1},{8,10},{10,12},{12... | collective-permute-start | bytes 196616 | tf_op jit(solution)/shard_map/ppermute | solution.py:25
  17.6 9.0 %collective-permute-start.7 = (bf16[8,4096]{1,0:T(8,128)(2,1)}, bf16[8,4096]{1,0:T(8,128)(2,1)S(1)}, u32[]{:S(2)}, u32[]{:S(2)}) collective-permute-start(bf16[8,4096]{1,0:T(8,128)(2,1)} %param.6), channel_id=1, source_target_pairs={{0,4},{2,6},{4,0},{6,2},{1,5},{3,7},{5,1},{7,3},{8,12},{10,14},{12... | collective-permute-start | bytes 196616 | tf_op jit(solution)/shard_map/ppermute | solution.py:25
  18.7 10.8 %collective-permute-start.8 = (bf16[8,4096]{1,0:T(8,128)(2,1)}, bf16[8,4096]{1,0:T(8,128)(2,1)S(1)}, u32[]{:S(2)}, u32[]{:S(2)}) collective-permute-start(bf16[8,4096]{1,0:T(8,128)(2,1)} %param.6), channel_id=1, source_target_pairs={{0,6},{2,0},{4,2},{6,4},{1,7},{3,1},{5,3},{7,5},{8,14},{10,8},{12,... | collective-permute-start | bytes 196616 | tf_op jit(solution)/shard_map/ppermute | solution.py:25
  22.4 11.5 %collective-permute-start = (bf16[16,4096]{1,0:T(8,128)(2,1)S(1)}, bf16[16,4096]{1,0:T(8,128)(2,1)S(1)}, u32[]{:S(2)}, u32[]{:S(2)}) collective-permute-start(bf16[16,4096]{1,0:T(8,128)(2,1)S(1)} %constant_dynamic-update-slice_fusion), channel_id=1, source_target_pairs={{0,128},{128,0},{1,129},{129,1},{2,130},{130,2},{3,131},{131,3},{4... | collective-permute-start | bytes 393224 | tf_op jit(solution)/shard_map/ppermute | solution.py:30
  25.0 6.8 %collective-permute-start.2 = (bf16[8,4096]{1,0:T(8,128)(2,1)S(1)}, bf16[8,4096]{1,0:T(8,128)(2,1)S(1)}, u32[]{:S(2)}, u32[]{:S(2)}) collective-permute-start(bf16[8,4096]{1,0:T(8,128)(2,1)S(1)} %slice.91), channel_id=1, source_target_pairs={{0,8},{8,16},{16,24},{24,0},{1,9},{9,17},{17,25},{25,1},{2,10},{10... | collective-permute-start | bytes 196616 | tf_op jit(solution)/shard_map/ppermute | solution.py:25
  26.6 5.8 %collective-permute-start.3 = (bf16[8,4096]{1,0:T(8,128)(2,1)S(1)}, bf16[8,4096]{1,0:T(8,128)(2,1)S(1)}, u32[]{:S(2)}, u32[]{:S(2)}) collective-permute-start(bf16[8,4096]{1,0:T(8,128)(2,1)S(1)} %slice.91), channel_id=1, source_target_pairs={{0,16},{8,24},{16,0},{24,8},{1,17},{9,25},{17,1},{25,9},{2,18},{10... | collective-permute-start | bytes 196616 | tf_op jit(solution)/shard_map/ppermute | solution.py:25
  29.6 4.3 %collective-permute-start.4 = (bf16[8,4096]{1,0:T(8,128)(2,1)S(1)}, bf16[8,4096]{1,0:T(8,128)(2,1)S(1)}, u32[]{:S(2)}, u32[]{:S(2)}) collective-permute-start(bf16[8,4096]{1,0:T(8,128)(2,1)S(1)} %slice.91), channel_id=1, source_target_pairs={{0,24},{8,0},{16,8},{24,16},{1,25},{9,1},{17,9},{25,17},{2,26},{10... | collective-permute-start | bytes 196616 | tf_op jit(solution)/shard_map/ppermute | solution.py:25
  34.0 0.8 copy-start.4
  36.7 9.6 %collective-permute-start.9 = (bf16[32,4096]{1,0:T(8,128)(2,1)S(1)}, bf16[32,4096]{1,0:T(8,128)(2,1)S(1)}, u32[]{:S(2)}, u32[]{:S(2)}) collective-permute-start(bf16[32,4096]{1,0:T(8,128)(2,1)S(1)} %pad_maximum_fusion.2), channel_id=1, source_target_pairs={{0,8},{8,16},{16,24},{24,0},{1,9},{9,17},{17,25},{25,1},{2,10},{10... | collective-permute-start | bytes 786440 | tf_op jit(solution)/shard_map/ppermute | solution.py:25
  37.0 12.0 %collective-permute-start.10 = (bf16[32,4096]{1,0:T(8,128)(2,1)S(1)}, bf16[32,4096]{1,0:T(8,128)(2,1)S(1)}, u32[]{:S(2)}, u32[]{:S(2)}) collective-permute-start(bf16[32,4096]{1,0:T(8,128)(2,1)S(1)} %pad_maximum_fusion.2), channel_id=1, source_target_pairs={{0,16},{8,24},{16,0},{24,8},{1,17},{9,25},{17,1},{25,9},{2,18},{10... | collective-permute-start | bytes 786440 | tf_op jit(solution)/shard_map/ppermute | solution.py:25
  40.7 8.5 %collective-permute-start.11 = (bf16[32,4096]{1,0:T(8,128)(2,1)S(1)}, bf16[32,4096]{1,0:T(8,128)(2,1)S(1)}, u32[]{:S(2)}, u32[]{:S(2)}) collective-permute-start(bf16[32,4096]{1,0:T(8,128)(2,1)S(1)} %pad_maximum_fusion.2), channel_id=1, source_target_pairs={{0,24},{8,0},{16,8},{24,16},{1,25},{9,1},{17,9},{25,17},{2,26},{10... | collective-permute-start | bytes 786440 | tf_op jit(solution)/shard_map/ppermute | solution.py:25
  40.8 8.5 %collective-permute-start.12 = (bf16[32,4096]{1,0:T(8,128)(2,1)S(1)}, bf16[32,4096]{1,0:T(8,128)(2,1)S(1)}, u32[]{:S(2)}, u32[]{:S(2)}) collective-permute-start(bf16[32,4096]{1,0:T(8,128)(2,1)S(1)} %pad_maximum_fusion.1), channel_id=1, source_target_pairs={{0,2},{2,4},{4,6},{6,0},{1,3},{3,5},{5,7},{7,1},{8,10},{10,12},{12... | collective-permute-start | bytes 786440 | tf_op jit(solution)/shard_map/ppermute | solution.py:25
  42.8 8.2 %collective-permute-start.13 = (bf16[32,4096]{1,0:T(8,128)(2,1)S(1)}, bf16[32,4096]{1,0:T(8,128)(2,1)S(1)}, u32[]{:S(2)}, u32[]{:S(2)}) collective-permute-start(bf16[32,4096]{1,0:T(8,128)(2,1)S(1)} %pad_maximum_fusion.1), channel_id=1, source_target_pairs={{0,4},{2,6},{4,0},{6,2},{1,5},{3,7},{5,1},{7,3},{8,12},{10,14},{12... | collective-permute-start | bytes 786440 | tf_op jit(solution)/shard_map/ppermute | solution.py:25
  46.2 9.5 %collective-permute-start.14 = (bf16[32,4096]{1,0:T(8,128)(2,1)S(1)}, bf16[32,4096]{1,0:T(8,128)(2,1)S(1)}, u32[]{:S(2)}, u32[]{:S(2)}) collective-permute-start(bf16[32,4096]{1,0:T(8,128)(2,1)S(1)} %pad_maximum_fusion.1), channel_id=1, source_target_pairs={{0,6},{2,0},{4,2},{6,4},{1,7},{3,1},{5,3},{7,5},{8,14},{10,8},{12,... | collective-permute-start | bytes 786440 | tf_op jit(solution)/shard_map/ppermute | solution.py:25
  55.8 6.7 %copy-start = (bf16[256,4096]{1,0:T(8,128)(2,1)}, bf16[256,4096]{1,0:T(8,128)(2,1)S(1)}, u32[]{:S(2)}) copy-start(bf16[256,4096]{1,0:T(8,128)(2,1)S(1)} %constant_dynamic-update-slice_fusion.3.rows_ref) | copy-start | bytes 6291460
  63.1 15.2 %copy-start.6 = (f32[3,256]{1,0:T(4,128)}, f32[3,256]{1,0:T(4,128)S(1)}, u32[]{:S(2)}) copy-start(f32[3,256]{1,0:T(4,128)S(1)} %fusion.20) | copy-start | bytes 9220
  64.1 30.1 %all-to-all-start = ((f32[32,3,256]{2,1,0:T(4,128)}), f32[32,3,256]{2,1,0:T(4,128)S(1)}, u32[]{:S(2)}, u32[]{:S(2)}) async-start(f32[32,3,256]{2,1,0:T(4,128)} %broadcast_in_dim.7), calls=%async_computation | async-start | bytes 262144 | tf_op jit(solution)/shard_map/all_to_all | solution.py:166
  76.6 16.4 %collective-permute-start.17 = (s32[2,256]{1,0:T(2,128)S(1)}, s32[2,256]{1,0:T(2,128)S(1)}, u32[]{:S(2)}, u32[]{:S(2)}) collective-permute-start(s32[2,256]{1,0:T(2,128)S(1)} %reshape.249), channel_id=1, source_target_pairs={{0,128},{128,0},{1,129},{129,1},{2,130},{130,2},{3,131},{131,3},{4... | collective-permute-start | bytes 6152 | tf_op jit(solution)/shard_map/ppermute | solution.py:30
  77.1 5.0 %copy-start.1 = (bf16[256,1024]{1,0:T(8,128)(2,1)}, bf16[256,1024]{1,0:T(8,128)(2,1)S(1)}, u32[]{:S(2)}) copy-start(bf16[256,1024]{1,0:T(8,128)(2,1)S(1)} %convolution_convert_fusion.weights_ref) | copy-start | bytes 1572868
  78.3 32.1 %collective-permute-start.15 = (bf16[256,512]{1,0:T(8,128)(2,1)}, bf16[256,512]{1,0:T(8,128)(2,1)}, u32[]{:S(2)}, u32[]{:S(2)}) collective-permute-start(bf16[256,512]{1,0:T(8,128)(2,1)} %convolution_convert_fusion.2), channel_id=1, source_target_pairs={{0,128},{128,0},{1,129},{129,1},{2,130},{130,2},{3,131},{131,3},{4... | collective-permute-start | bytes 786440 | tf_op jit(solution)/shard_map/ppermute | solution.py:30
  82.1 13.2 %slice-start = ((f32[3,256]{1,0:T(4,128)}), f32[1,256]{1,0:T(1,128)S(1)}, s32[]{:S(2)}) async-start(f32[3,256]{1,0:T(4,128)} %copy-done.6), calls=%async_computation.3 | async-start | bytes 2048 | tf_op jit(solution)/shard_map/slice | solution.py:199
  100.4 9.9 %collective-permute-start.16 = (f32[256]{0:T(256)S(1)}, f32[256]{0:T(256)S(1)}, u32[]{:S(2)}, u32[]{:S(2)}) collective-permute-start(f32[256]{0:T(256)S(1)} %subtract_exponential_fusion), channel_id=1, source_target_pairs={{0,128},{128,0},{1,129},{129,1},{2,130},{130,2},{3,131},{131,3},{4... | collective-permute-start | bytes 3080 | tf_op jit(solution)/shard_map/ppermute | solution.py:30
  100.7 30.5 %all-to-all-start.1 = ((bf16[16,16,4096]{2,1,0:T(8,128)(2,1)}), bf16[16,16,4096]{2,1,0:T(8,128)(2,1)S(1)}, u32[]{:S(2)}, u32[]{:S(2)}) async-start(bf16[16,16,4096]{2,1,0:T(8,128)(2,1)} %bitcast.13), calls=%async_computation.1 | async-start | bytes 4194304 | tf_op jit(solution)/shard_map/all_to_all | solution.py:205
  124.6 3.5 %collective-permute-start.20 = (bf16[256,2048]{1,0:T(8,128)(2,1)}, bf16[256,2048]{1,0:T(8,128)(2,1)S(1)}, u32[]{:S(2)}, u32[]{:S(2)}) collective-permute-start(bf16[256,2048]{1,0:T(8,128)(2,1)} %get-tuple-element.47), channel_id=1, source_target_pairs={{0,32},{32,0},{1,33},{33,1},{2,34},{34,2},{3,35},{35,3},{4,36},{36... | collective-permute-start | bytes 3145736 | tf_op jit(solution)/shard_map/ppermute | solution.py:30
  124.6 12.4 %collective-permute-start.18 = (bf16[256,2048]{1,0:T(8,128)(2,1)}, bf16[256,2048]{1,0:T(8,128)(2,1)}, u32[]{:S(2)}, u32[]{:S(2)}) collective-permute-start(bf16[256,2048]{1,0:T(8,128)(2,1)} %get-tuple-element.44), channel_id=1, source_target_pairs={{0,32},{32,0},{1,33},{33,1},{2,34},{34,2},{3,35},{35,3},{4,36},{36... | collective-permute-start | bytes 3145736 | tf_op jit(solution)/shard_map/ppermute | solution.py:30
  130.2 32.3 %collective-permute-start.21 = (bf16[128,2048]{1,0:T(8,128)(2,1)}, bf16[128,2048]{1,0:T(8,128)(2,1)}, u32[]{:S(2)}, u32[]{:S(2)}) collective-permute-start(bf16[128,2048]{1,0:T(8,128)(2,1)} %add_convert_fusion), channel_id=1, source_target_pairs={{0,64},{64,0},{1,65},{65,1},{2,66},{66,2},{3,67},{67,3},{4,68},{68... | collective-permute-start | bytes 1572872 | tf_op jit(solution)/shard_map/ppermute | solution.py:30
  131.2 5.7 %copy-start.3 = (f32[256,2048]{1,0:T(8,128)S(1)}, f32[256,2048]{1,0:T(8,128)}, u32[]{:S(2)}) copy-start(f32[256,2048]{1,0:T(8,128)} %get-tuple-element.43) | copy-start | bytes 6291460
  131.5 23.6 %collective-permute-start.22 = (f32[8,4096]{1,0:T(8,128)S(1)}, f32[8,4096]{1,0:T(8,128)S(1)}, u32[]{:S(2)}, u32[]{:S(2)}) collective-permute-start(f32[8,4096]{1,0:T(8,128)S(1)} %slice_bitcast_fusion), channel_id=1, source_target_pairs={{0,1},{1,0},{2,3},{3,2},{4,5},{5,4},{6,7},{7,6},{8,9},{9,8},{10,11... | collective-permute-start | bytes 393224 | tf_op jit(solution)/shard_map/ppermute | solution.py:30
  138.1 24.4 %copy-start.2 = (f32[256,2048]{1,0:T(8,128)S(1)}, f32[256,2048]{1,0:T(8,128)}, u32[]{:S(2)}) copy-start(f32[256,2048]{1,0:T(8,128)} %get-tuple-element.46) | copy-start | bytes 6291460
  138.1 23.1 %collective-permute-start.19 = (bf16[128,2048]{1,0:T(8,128)(2,1)S(1)}, bf16[128,2048]{1,0:T(8,128)(2,1)S(1)}, u32[]{:S(2)}, u32[]{:S(2)}) collective-permute-start(bf16[128,2048]{1,0:T(8,128)(2,1)S(1)} %add_convert_fusion.1), channel_id=1, source_target_pairs={{0,64},{64,0},{1,65},{65,1},{2,66},{66,2},{3,67},{67,3},{4,68},{68... | collective-permute-start | bytes 1572872 | tf_op jit(solution)/shard_map/ppermute | solution.py:30
Sparse Core Ops, SparseCore 0:
  34.9 71.2 all-gather.1

commit v3 on v2

--- a/solution.py
+++ b/solution.py
@@ -41,7 +41,7 @@
 def hidden_product(weights, hit, table):
     tokens, depth = weights.shape
     columns = table.shape[1]
-    tile = min(512, columns)
+    tile = min(1024, columns)
     still = pl.BlockSpec((tokens, depth), lambda i: (0, 0))
     out = pl.BlockSpec((tokens, tile), lambda i: (0, i))
     return pl.pallas_call(
@@ -77,7 +77,7 @@
     tokens, out_rows = own.shape
     depth = more.shape[0]
     chips = lax.axis_size(("y", "x"))
-    tile = min(512, columns)
+    tile = min(1024, columns)
     begin = at_column // tile
     still = lambda i: (0, 0)
     moving = lambda i: (0, begin + i)

time: 175 us -> 180 us (1.029)
  the two profiles are of different devices: /device:TPU:2 before, /device:TPU:76 now
where the time goes in v3:
time: 180 us; the launch traced here: 179 us
  starting transfers between devices  55.8 us (31%)
  waiting for transfers between devices  49.8 us (28%)
  other arithmetic  21.7 us (12%)
  Pallas kernels  20.4 us (11%)
  between operations  14.5 us (8%)
  matrix products  11.4 us (6%)
  local copies, waits for them, and re-layouts  5.83 us (3%)
    ppermute x10, waiting for transfers between devices, swap(): return lax.ppermute(array, axis, [(i, n - 1 - i) for i in range(n)])  32.1 us
    ppermute x10, starting transfers between devices, swap(): return lax.ppermute(array, axis, [(i, n - 1 - i) for i in range(n)])  21.3 us
    ppermute x12, starting transfers between devices, shift(): return lax.ppermute(array, axis, [(i, (i + by) % n) for i in range(n)])  16.5 us
    ppermute x12, waiting for transfers between devices, shift(): return lax.ppermute(array, axis, [(i, (i + by) % n) for i in range(n)])  13.3 us
    pallas_call x2, Pallas kernels, table_product(): pl.pallas_call(functools.partial(table_product_kernel, chips), grid=(colu...  11.2 us
    all_to_all x1, starting transfers between devices, shards(): everyone = lax.all_to_all(mine_all, VOCAB, 0, 0, tiled=True)  10.7 us
    pallas_call x1, Pallas kernels, hidden_product(): pl.pallas_call(hidden_product_kernel, grid=(columns // tile,), in_specs=[...  9.2 us
    all_to_all x1, starting transfers between devices, shards(): partial = lax.all_to_all(partial, ('y', 'x'), 0, 0, tiled=True)  7.28 us
  transfers between devices with their start and end apart: 26, of which 11 were waited for; matrix products, arithmetic and copies ran while one was open for 18% of the time, Pallas kernels for 11%

profile of v3, /device:TPU:76, one launch (start us, length us, event | category | flops | bytes accessed | tf_op | source)
XLA Modules:
  0.0 179.3 jit_solution(3563322392474661578)
XLA Ops:
  7.2 0.8 constant_dynamic-update-slice_fusion.1
  8.1 0.8 constant_dynamic-update-slice_fusion
  8.9 5.4 %collective-permute-start.1 = (bf16[16,4096]{1,0:T(8,128)(2,1)S(1)}, bf16[16,4096]{1,0:T(8,128)(2,1)S(1)}, u32[]{:S(2)}, u32[]{:S(2)}) collective-permute-start(bf16[16,4096]{1,0:T(8,128)(2,1)S(1)} %constant_dynamic-update-slice_fusion), channel_id=1, source_target_pairs={{0,1},{1,0},{2,3},{3,2},{4,5},{5,4},{6,7},{7,6},{8,9},{9,8},{10,11... | collective-permute-start | bytes 393224 | tf_op jit(solution)/shard_map/ppermute | solution.py:30
  14.3 1.2 collective-permute-start.6
  15.5 0.8 collective-permute-start.7
  16.3 1.1 collective-permute-start.8
  18.9 3.3 %collective-permute-done.1 = bf16[16,4096]{1,0:T(8,128)(2,1)S(1)} collective-permute-done((bf16[16,4096]{1,0:T(8,128)(2,1)S(1)}, bf16[16,4096]{1,0:T(8,128)(2,1)S(1)}, u32[]{:S(2)}, u32[]{:S(2)}) %collective-permute-start.1) | collective-permute-done | bytes 131104 | tf_op jit(solution)/shard_map/ppermute | solution.py:30
  22.2 1.7 collective-permute-start.2
  23.9 0.9 collective-permute-start.3
  24.8 2.4 %collective-permute-start.4 = (bf16[8,4096]{1,0:T(8,128)(2,1)S(1)}, bf16[8,4096]{1,0:T(8,128)(2,1)S(1)}, u32[]{:S(2)}, u32[]{:S(2)}) collective-permute-start(bf16[8,4096]{1,0:T(8,128)(2,1)S(1)} %slice.91), channel_id=1, source_target_pairs={{0,24},{8,0},{16,8},{24,16},{1,25},{9,1},{17,9},{25,17},{2,26},{10... | collective-permute-start | bytes 196616 | tf_op jit(solution)/shard_map/ppermute | solution.py:25
  27.2 0.9 pad_maximum_fusion.2
  28.1 1.7 collective-permute-done.3
  29.9 0.8 copy-done.4
  30.9 1.8 fusion
  32.6 1.1 collective-permute-start.9
  33.8 2.6 %collective-permute-start.10 = (bf16[32,4096]{1,0:T(8,128)(2,1)S(1)}, bf16[32,4096]{1,0:T(8,128)(2,1)S(1)}, u32[]{:S(2)}, u32[]{:S(2)}) collective-permute-start(bf16[32,4096]{1,0:T(8,128)(2,1)S(1)} %pad_maximum_fusion.2), channel_id=1, source_target_pairs={{0,16},{8,24},{16,0},{24,8},{1,17},{9,25},{17,1},{25,9},{2,18},{10... | collective-permute-start | bytes 786440 | tf_op jit(solution)/shard_map/ppermute | solution.py:25
  36.4 2.0 %collective-permute-start.11 = (bf16[32,4096]{1,0:T(8,128)(2,1)S(1)}, bf16[32,4096]{1,0:T(8,128)(2,1)S(1)}, u32[]{:S(2)}, u32[]{:S(2)}) collective-permute-start(bf16[32,4096]{1,0:T(8,128)(2,1)S(1)} %pad_maximum_fusion.2), channel_id=1, source_target_pairs={{0,24},{8,0},{16,8},{24,16},{1,25},{9,1},{17,9},{25,17},{2,26},{10... | collective-permute-start | bytes 786440 | tf_op jit(solution)/shard_map/ppermute | solution.py:25
  38.4 1.2 collective-permute-start.12
  40.3 1.6 collective-permute-done.9
  42.6 1.9 %collective-permute-done.10 = bf16[32,4096]{1,0:T(8,128)(2,1)S(1)} collective-permute-done((bf16[32,4096]{1,0:T(8,128)(2,1)S(1)}, bf16[32,4096]{1,0:T(8,128)(2,1)S(1)}, u32[]{:S(2)}, u32[]{:S(2)}) %collective-permute-start.10) | collective-permute-done | bytes 262176 | tf_op jit(solution)/shard_map/ppermute | solution.py:25
  44.5 3.3 %collective-permute-done.11 = bf16[32,4096]{1,0:T(8,128)(2,1)S(1)} collective-permute-done((bf16[32,4096]{1,0:T(8,128)(2,1)S(1)}, bf16[32,4096]{1,0:T(8,128)(2,1)S(1)}, u32[]{:S(2)}, u32[]{:S(2)}) %collective-permute-start.11) | collective-permute-done | bytes 262176 | tf_op jit(solution)/shard_map/ppermute | solution.py:25
  48.0 2.0 %collective-permute-done.13 = bf16[32,4096]{1,0:T(8,128)(2,1)S(1)} collective-permute-done((bf16[32,4096]{1,0:T(8,128)(2,1)S(1)}, bf16[32,4096]{1,0:T(8,128)(2,1)S(1)}, u32[]{:S(2)}, u32[]{:S(2)}) %collective-permute-start.13) | collective-permute-done | bytes 262176 | tf_op jit(solution)/shard_map/ppermute | solution.py:25
  50.0 2.8 %collective-permute-done.14 = bf16[32,4096]{1,0:T(8,128)(2,1)S(1)} collective-permute-done((bf16[32,4096]{1,0:T(8,128)(2,1)S(1)}, bf16[32,4096]{1,0:T(8,128)(2,1)S(1)}, u32[]{:S(2)}, u32[]{:S(2)}) %collective-permute-start.14) | collective-permute-done | bytes 262176 | tf_op jit(solution)/shard_map/ppermute | solution.py:25
  52.8 6.7 %fusion.43 = (f32[256]{0:T(256)S(1)}, f32[256,1024]{1,0:T(8,128)S(1)}) fusion(bf16[256,4096]{1,0:T(8,128)(2,1)S(1)} %constant_dynamic-update-slice_fusion.3.rows_ref, bf16[1024,4096]{1,0:T(8,128)(2,1)} %table_ref.1), kind=kOutput, calls=%fused_computation.133 | convolution fusion | flops 2147745536 | bytes 11535360 | tf_op jit(solution)/shard_map/dot_general | solution.py:158
  61.2 10.7 %all-to-all-start = ((f32[32,3,256]{2,1,0:T(4,128)}), f32[32,3,256]{2,1,0:T(4,128)S(1)}, u32[]{:S(2)}, u32[]{:S(2)}) async-start(f32[32,3,256]{2,1,0:T(4,128)} %broadcast_in_dim.7), calls=%async_computation | async-start | bytes 262144 | tf_op jit(solution)/shard_map/all_to_all | solution.py:166
  71.9 4.3 %collective-permute-start.17 = (s32[2,256]{1,0:T(2,128)S(1)}, s32[2,256]{1,0:T(2,128)S(1)}, u32[]{:S(2)}, u32[]{:S(2)}) collective-permute-start(s32[2,256]{1,0:T(2,128)S(1)} %reshape.249), channel_id=1, source_target_pairs={{0,128},{128,0},{1,129},{129,1},{2,130},{130,2},{3,131},{131,3},{4... | collective-permute-start | bytes 6152 | tf_op jit(solution)/shard_map/ppermute | solution.py:30
  76.6 1.2 convolution_convert_fusion.2
  77.8 0.9 compare_convert_fusion.1.hit_ref
  78.7 9.2 %shard_map.76 = (f32[256,4096]{1,0:T(8,128)}, bf16[256,4096]{1,0:T(8,128)(2,1)}) custom-call(bf16[256,1024]{1,0:T(8,128)(2,1)} %copy-done.1, bf16[256,1024]{1,0:T(8,128)(2,1)} %compare_convert_fusion.1.hit_ref, bf16[1024,4096]{1,0:T(8,128)(2,1)} %table_ref.1), custom_call_target="tpu_custom_call" | custom-call | flops 4294967296 | bytes 15728640 | tf_op jit(solution)/shard_map/pallas_call | solution.py:47
  88.3 0.9 add_convert_fusion.2
  90.3 5.1 %subtract_convert_fusion = bf16[256,4096]{1,0:T(8,128)(2,1)} fusion(bf16[256,4096]{1,0:T(8,128)(2,1)} %get-tuple-element.38, f32[256,4096]{1,0:T(8,128)} %get-tuple-element.37, f32[256]{0:T(256)S(1)} %subtract_exponential_fusion), kind=kLoop, calls=%fused_computation.1 | loop fusion | flops 4194304 | bytes 8389632 | tf_op jit(solution)/shard_map/convert_element_type | solution.py:202
  95.4 2.9 %collective-permute-start.16 = (f32[256]{0:T(256)S(1)}, f32[256]{0:T(256)S(1)}, u32[]{:S(2)}, u32[]{:S(2)}) collective-permute-start(f32[256]{0:T(256)S(1)} %subtract_exponential_fusion), channel_id=1, source_target_pairs={{0,128},{128,0},{1,129},{129,1},{2,130},{130,2},{3,131},{131,3},{4... | collective-permute-start | bytes 3080 | tf_op jit(solution)/shard_map/ppermute | solution.py:30
  98.6 7.3 %all-to-all-start.1 = ((bf16[16,16,4096]{2,1,0:T(8,128)(2,1)}), bf16[16,16,4096]{2,1,0:T(8,128)(2,1)S(1)}, u32[]{:S(2)}, u32[]{:S(2)}) async-start(bf16[16,16,4096]{2,1,0:T(8,128)(2,1)} %bitcast.13), calls=%async_computation.1 | async-start | bytes 4194304 | tf_op jit(solution)/shard_map/all_to_all | solution.py:205
  105.9 2.4 %convolution_convert_fusion.1.own_ref = bf16[256,512]{1,0:T(8,128)(2,1)} fusion(bf16[1024,512]{1,0:T(8,128)(2,1)} %get-tuple-element.40, f32[256,1024]{1,0:T(8,128)S(1)} %get-tuple-element.67, f32[256]{0:T(256)S(1)} %bitcast.75, s32[1024]{0:T(1024)S(1)} %iota_add_fusion, s32[256]{0:T(256)S(1)} %convert_element_type.98), kind=kOutput, calls=%fused_computation.10 | convolution fusion | flops 269877248 | bytes 2365440 | tf_op jit(solution)/shard_map/dot_general | solution.py:181
  108.3 1.8 %subtract_convert_fusion.1.other_ref = bf16[256,512]{1,0:T(8,128)(2,1)} fusion(bf16[256,512]{1,0:T(8,128)(2,1)} %collective-permute-done.15, s32[512]{0:T(512)S(1)} %get-tuple-element.63, f32[256]{0:T(256)S(1)} %collective-permute-done.16, s32[256]{0:T(256)S(1)} %bitcast.71), kind=kLoop, calls=%fused_computation.23 | loop fusion | flops 786432 | bytes 528384 | tf_op jit(solution)/shard_map/convert_element_type | solution.py:210
  110.2 4.3 %all-gather.2.cloned.1.call-done.more_ref = bf16[768,4096]{1,0:T(8,128)(2,1)} async-done(((bf16[48,4096]{1,0:T(8,128)(2,1)}), bf16[768,4096]{1,0:T(8,128)(2,1)}) %all-gather.2.cloned.1.call-update) | async-done | bytes 6291472 | tf_op jit(solution)/shard_map/all_gather | solution.py:154
  114.5 5.6 %shard_map.77 = (f32[256,2048]{1,0:T(8,128)}, bf16[256,2048]{1,0:T(8,128)(2,1)}) custom-call(bf16[256,512]{1,0:T(8,128)(2,1)} %convolution_convert_fusion.1.own_ref, bf16[256,512]{1,0:T(8,128)(2,1)} %subtract_convert_fusion.1.other_ref, bf16[512,512]{1,0:T(8,128)(2,1)} %bitcast.55, bf16[256,4096]{1,0:T(8,128)(2,1)} %copy-done, ...), custom_call_target="tpu_custom_call" | custom-call | flops 2147483648 | bytes 8388608 | tf_op jit(solution)/shard_map/pallas_call | solution.py:84
  120.0 5.6 %shard_map.78 = (f32[256,2048]{1,0:T(8,128)}, bf16[256,2048]{1,0:T(8,128)(2,1)}) custom-call(bf16[256,512]{1,0:T(8,128)(2,1)} %convolution_convert_fusion.1.own_ref, bf16[256,512]{1,0:T(8,128)(2,1)} %subtract_convert_fusion.1.other_ref, bf16[512,512]{1,0:T(8,128)(2,1)} %bitcast.56, bf16[256,4096]{1,0:T(8,128)(2,1)} %copy-done, ...), custom_call_target="tpu_custom_call" | custom-call | flops 2147483648 | bytes 8388608 | tf_op jit(solution)/shard_map/pallas_call | solution.py:84
  126.2 3.0 %collective-permute-done.20 = bf16[256,2048]{1,0:T(8,128)(2,1)S(1)} collective-permute-done((bf16[256,2048]{1,0:T(8,128)(2,1)}, bf16[256,2048]{1,0:T(8,128)(2,1)S(1)}, u32[]{:S(2)}, u32[]{:S(2)}) %collective-permute-start.20) | collective-permute-done | bytes 1048608 | tf_op jit(solution)/shard_map/ppermute | solution.py:30
  129.2 2.1 %add_convert_fusion = bf16[128,2048]{1,0:T(8,128)(2,1)} fusion(f32[256,2048]{1,0:T(8,128)} %get-tuple-element.46, bf16[256,2048]{1,0:T(8,128)(2,1)S(1)} %collective-permute-done.20), kind=kLoop, calls=%fused_computation.16 | loop fusion | flops 786432 | bytes 2097152 | tf_op jit(solution)/shard_map/convert_element_type | solution.py:219
  131.3 8.0 %collective-permute-start.21 = (bf16[128,2048]{1,0:T(8,128)(2,1)}, bf16[128,2048]{1,0:T(8,128)(2,1)}, u32[]{:S(2)}, u32[]{:S(2)}) collective-permute-start(bf16[128,2048]{1,0:T(8,128)(2,1)} %add_convert_fusion), channel_id=1, source_target_pairs={{0,64},{64,0},{1,65},{65,1},{2,66},{66,2},{3,67},{67,3},{4,68},{68... | collective-permute-start | bytes 1572872 | tf_op jit(solution)/shard_map/ppermute | solution.py:30
  139.7 1.2 copy-done.3
  140.9 1.2 add_convert_fusion.1
  142.1 15.2 %collective-permute-done.22 = f32[8,4096]{1,0:T(8,128)S(1)} collective-permute-done((f32[8,4096]{1,0:T(8,128)S(1)}, f32[8,4096]{1,0:T(8,128)S(1)}, u32[]{:S(2)}, u32[]{:S(2)}) %collective-permute-start.22) | collective-permute-done | bytes 131104 | tf_op jit(solution)/shard_map/ppermute | solution.py:30
  158.0 10.5 %collective-permute-done.19 = bf16[128,2048]{1,0:T(8,128)(2,1)S(1)} collective-permute-done((bf16[128,2048]{1,0:T(8,128)(2,1)S(1)}, bf16[128,2048]{1,0:T(8,128)(2,1)S(1)}, u32[]{:S(2)}, u32[]{:S(2)}) %collective-permute-start.19) | collective-permute-done | bytes 524320 | tf_op jit(solution)/shard_map/ppermute | solution.py:30
  168.6 1.2 convert_add_fusion.1
  169.8 1.2 convert_add_fusion
  171.0 1.5 pad_maximum_fusion
  (96 shorter events, 8.8 us)
Async XLA Ops:
  7.2 22.7 %copy-start.5 = (bf16[8,4096]{1,0:T(8,128)(2,1)S(1)}, bf16[8,4096]{1,0:T(8,128)(2,1)}, u32[]{:S(2)}) copy-start(bf16[8,4096]{1,0:T(8,128)(2,1)} %param.7) | copy-start | bytes 196612
  7.2 107.3 %all-gather.2.cloned.1.call-start = ((), (), s32[]{:S(2)}) async-start(), calls=%async_computation.2 | async-start | bytes 6684672 | tf_op jit(solution)/shard_map/all_gather | solution.py:154
  8.9 13.3 %collective-permute-start.1 = (bf16[16,4096]{1,0:T(8,128)(2,1)S(1)}, bf16[16,4096]{1,0:T(8,128)(2,1)S(1)}, u32[]{:S(2)}, u32[]{:S(2)}) collective-permute-start(bf16[16,4096]{1,0:T(8,128)(2,1)S(1)} %constant_dynamic-update-slice_fusion), channel_id=1, source_target_pairs={{0,1},{1,0},{2,3},{3,2},{4,5},{5,4},{6,7},{7,6},{8,9},{9,8},{10,11... | collective-permute-start | bytes 393224 | tf_op jit(solution)/shard_map/ppermute | solution.py:30
  14.3 15.5 %collective-permute-start.5 = (bf16[16,4096]{1,0:T(8,128)(2,1)S(1)}, bf16[16,4096]{1,0:T(8,128)(2,1)S(1)}, u32[]{:S(2)}, u32[]{:S(2)}) collective-permute-start(bf16[16,4096]{1,0:T(8,128)(2,1)S(1)} %constant_dynamic-update-slice_fusion), channel_id=1, source_target_pairs={{0,129},{129,0},{1,128},{128,1},{2,131},{131,2},{3,130},{130,3},{4... | collective-permute-start | bytes 393224 | tf_op jit(solution)/shard_map/ppermute | solution.py:145
  14.3 7.9 %collective-permute-start.6 = (bf16[8,4096]{1,0:T(8,128)(2,1)}, bf16[8,4096]{1,0:T(8,128)(2,1)S(1)}, u32[]{:S(2)}, u32[]{:S(2)}) collective-permute-start(bf16[8,4096]{1,0:T(8,128)(2,1)} %param.6), channel_id=1, source_target_pairs={{0,2},{2,4},{4,6},{6,0},{1,3},{3,5},{5,7},{7,1},{8,10},{10,12},{12... | collective-permute-start | bytes 196616 | tf_op jit(solution)/shard_map/ppermute | solution.py:25
  15.5 8.3 %collective-permute-start.7 = (bf16[8,4096]{1,0:T(8,128)(2,1)}, bf16[8,4096]{1,0:T(8,128)(2,1)S(1)}, u32[]{:S(2)}, u32[]{:S(2)}) collective-permute-start(bf16[8,4096]{1,0:T(8,128)(2,1)} %param.6), channel_id=1, source_target_pairs={{0,4},{2,6},{4,0},{6,2},{1,5},{3,7},{5,1},{7,3},{8,12},{10,14},{12... | collective-permute-start | bytes 196616 | tf_op jit(solution)/shard_map/ppermute | solution.py:25
  16.3 8.5 %collective-permute-start.8 = (bf16[8,4096]{1,0:T(8,128)(2,1)}, bf16[8,4096]{1,0:T(8,128)(2,1)S(1)}, u32[]{:S(2)}, u32[]{:S(2)}) collective-permute-start(bf16[8,4096]{1,0:T(8,128)(2,1)} %param.6), channel_id=1, source_target_pairs={{0,6},{2,0},{4,2},{6,4},{1,7},{3,1},{5,3},{7,5},{8,14},{10,8},{12,... | collective-permute-start | bytes 196616 | tf_op jit(solution)/shard_map/ppermute | solution.py:25
  22.2 7.6 %collective-permute-start = (bf16[16,4096]{1,0:T(8,128)(2,1)S(1)}, bf16[16,4096]{1,0:T(8,128)(2,1)S(1)}, u32[]{:S(2)}, u32[]{:S(2)}) collective-permute-start(bf16[16,4096]{1,0:T(8,128)(2,1)S(1)} %constant_dynamic-update-slice_fusion), channel_id=1, source_target_pairs={{0,128},{128,0},{1,129},{129,1},{2,130},{130,2},{3,131},{131,3},{4... | collective-permute-start | bytes 393224 | tf_op jit(solution)/shard_map/ppermute | solution.py:30
  22.2 5.9 %collective-permute-start.2 = (bf16[8,4096]{1,0:T(8,128)(2,1)S(1)}, bf16[8,4096]{1,0:T(8,128)(2,1)S(1)}, u32[]{:S(2)}, u32[]{:S(2)}) collective-permute-start(bf16[8,4096]{1,0:T(8,128)(2,1)S(1)} %slice.91), channel_id=1, source_target_pairs={{0,8},{8,16},{16,24},{24,0},{1,9},{9,17},{17,25},{25,1},{2,10},{10... | collective-permute-start | bytes 196616 | tf_op jit(solution)/shard_map/ppermute | solution.py:25
  23.9 5.9 %collective-permute-start.3 = (bf16[8,4096]{1,0:T(8,128)(2,1)S(1)}, bf16[8,4096]{1,0:T(8,128)(2,1)S(1)}, u32[]{:S(2)}, u32[]{:S(2)}) collective-permute-start(bf16[8,4096]{1,0:T(8,128)(2,1)S(1)} %slice.91), channel_id=1, source_target_pairs={{0,16},{8,24},{16,0},{24,8},{1,17},{9,25},{17,1},{25,9},{2,18},{10... | collective-permute-start | bytes 196616 | tf_op jit(solution)/shard_map/ppermute | solution.py:25
  24.8 5.0 %collective-permute-start.4 = (bf16[8,4096]{1,0:T(8,128)(2,1)S(1)}, bf16[8,4096]{1,0:T(8,128)(2,1)S(1)}, u32[]{:S(2)}, u32[]{:S(2)}) collective-permute-start(bf16[8,4096]{1,0:T(8,128)(2,1)S(1)} %slice.91), channel_id=1, source_target_pairs={{0,24},{8,0},{16,8},{24,16},{1,25},{9,1},{17,9},{25,17},{2,26},{10... | collective-permute-start | bytes 196616 | tf_op jit(solution)/shard_map/ppermute | solution.py:25
  29.9 0.8 copy-start.4
  32.6 9.2 %collective-permute-start.9 = (bf16[32,4096]{1,0:T(8,128)(2,1)S(1)}, bf16[32,4096]{1,0:T(8,128)(2,1)S(1)}, u32[]{:S(2)}, u32[]{:S(2)}) collective-permute-start(bf16[32,4096]{1,0:T(8,128)(2,1)S(1)} %pad_maximum_fusion.2), channel_id=1, source_target_pairs={{0,8},{8,16},{16,24},{24,0},{1,9},{9,17},{17,25},{25,1},{2,10},{10... | collective-permute-start | bytes 786440 | tf_op jit(solution)/shard_map/ppermute | solution.py:25
  33.8 10.7 %collective-permute-start.10 = (bf16[32,4096]{1,0:T(8,128)(2,1)S(1)}, bf16[32,4096]{1,0:T(8,128)(2,1)S(1)}, u32[]{:S(2)}, u32[]{:S(2)}) collective-permute-start(bf16[32,4096]{1,0:T(8,128)(2,1)S(1)} %pad_maximum_fusion.2), channel_id=1, source_target_pairs={{0,16},{8,24},{16,0},{24,8},{1,17},{9,25},{17,1},{25,9},{2,18},{10... | collective-permute-start | bytes 786440 | tf_op jit(solution)/shard_map/ppermute | solution.py:25
  36.4 11.5 %collective-permute-start.11 = (bf16[32,4096]{1,0:T(8,128)(2,1)S(1)}, bf16[32,4096]{1,0:T(8,128)(2,1)S(1)}, u32[]{:S(2)}, u32[]{:S(2)}) collective-permute-start(bf16[32,4096]{1,0:T(8,128)(2,1)S(1)} %pad_maximum_fusion.2), channel_id=1, source_target_pairs={{0,24},{8,0},{16,8},{24,16},{1,25},{9,1},{17,9},{25,17},{2,26},{10... | collective-permute-start | bytes 786440 | tf_op jit(solution)/shard_map/ppermute | solution.py:25
  38.4 9.6 %collective-permute-start.12 = (bf16[32,4096]{1,0:T(8,128)(2,1)S(1)}, bf16[32,4096]{1,0:T(8,128)(2,1)S(1)}, u32[]{:S(2)}, u32[]{:S(2)}) collective-permute-start(bf16[32,4096]{1,0:T(8,128)(2,1)S(1)} %pad_maximum_fusion.1), channel_id=1, source_target_pairs={{0,2},{2,4},{4,6},{6,0},{1,3},{3,5},{5,7},{7,1},{8,10},{10,12},{12... | collective-permute-start | bytes 786440 | tf_op jit(solution)/shard_map/ppermute | solution.py:25
  39.6 10.4 %collective-permute-start.13 = (bf16[32,4096]{1,0:T(8,128)(2,1)S(1)}, bf16[32,4096]{1,0:T(8,128)(2,1)S(1)}, u32[]{:S(2)}, u32[]{:S(2)}) collective-permute-start(bf16[32,4096]{1,0:T(8,128)(2,1)S(1)} %pad_maximum_fusion.1), channel_id=1, source_target_pairs={{0,4},{2,6},{4,0},{6,2},{1,5},{3,7},{5,1},{7,3},{8,12},{10,14},{12... | collective-permute-start | bytes 786440 | tf_op jit(solution)/shard_map/ppermute | solution.py:25
  41.9 10.9 %collective-permute-start.14 = (bf16[32,4096]{1,0:T(8,128)(2,1)S(1)}, bf16[32,4096]{1,0:T(8,128)(2,1)S(1)}, u32[]{:S(2)}, u32[]{:S(2)}) collective-permute-start(bf16[32,4096]{1,0:T(8,128)(2,1)S(1)} %pad_maximum_fusion.1), channel_id=1, source_target_pairs={{0,6},{2,0},{4,2},{6,4},{1,7},{3,1},{5,3},{7,5},{8,14},{10,8},{12,... | collective-permute-start | bytes 786440 | tf_op jit(solution)/shard_map/ppermute | solution.py:25
  52.8 6.7 %copy-start = (bf16[256,4096]{1,0:T(8,128)(2,1)}, bf16[256,4096]{1,0:T(8,128)(2,1)S(1)}, u32[]{:S(2)}) copy-start(bf16[256,4096]{1,0:T(8,128)(2,1)S(1)} %constant_dynamic-update-slice_fusion.3.rows_ref) | copy-start | bytes 6291460
  60.1 17.7 %copy-start.6 = (f32[3,256]{1,0:T(4,128)}, f32[3,256]{1,0:T(4,128)S(1)}, u32[]{:S(2)}) copy-start(f32[3,256]{1,0:T(4,128)S(1)} %fusion.20) | copy-start | bytes 9220
  61.2 28.1 %all-to-all-start = ((f32[32,3,256]{2,1,0:T(4,128)}), f32[32,3,256]{2,1,0:T(4,128)S(1)}, u32[]{:S(2)}, u32[]{:S(2)}) async-start(f32[32,3,256]{2,1,0:T(4,128)} %broadcast_in_dim.7), calls=%async_computation | async-start | bytes 262144 | tf_op jit(solution)/shard_map/all_to_all | solution.py:166
  71.9 16.1 %collective-permute-start.17 = (s32[2,256]{1,0:T(2,128)S(1)}, s32[2,256]{1,0:T(2,128)S(1)}, u32[]{:S(2)}, u32[]{:S(2)}) collective-permute-start(s32[2,256]{1,0:T(2,128)S(1)} %reshape.249), channel_id=1, source_target_pairs={{0,128},{128,0},{1,129},{129,1},{2,130},{130,2},{3,131},{131,3},{4... | collective-permute-start | bytes 6152 | tf_op jit(solution)/shard_map/ppermute | solution.py:30
  76.6 2.1 %copy-start.1 = (bf16[256,1024]{1,0:T(8,128)(2,1)}, bf16[256,1024]{1,0:T(8,128)(2,1)S(1)}, u32[]{:S(2)}) copy-start(bf16[256,1024]{1,0:T(8,128)(2,1)S(1)} %convolution_convert_fusion.weights_ref) | copy-start | bytes 1572868
  77.8 30.6 %collective-permute-start.15 = (bf16[256,512]{1,0:T(8,128)(2,1)}, bf16[256,512]{1,0:T(8,128)(2,1)}, u32[]{:S(2)}, u32[]{:S(2)}) collective-permute-start(bf16[256,512]{1,0:T(8,128)(2,1)} %convolution_convert_fusion.2), channel_id=1, source_target_pairs={{0,128},{128,0},{1,129},{129,1},{2,130},{130,2},{3,131},{131,3},{4... | collective-permute-start | bytes 786440 | tf_op jit(solution)/shard_map/ppermute | solution.py:30
  78.7 11.6 %slice-start = ((f32[3,256]{1,0:T(4,128)}), f32[1,256]{1,0:T(1,128)S(1)}, s32[]{:S(2)}) async-start(f32[3,256]{1,0:T(4,128)} %copy-done.6), calls=%async_computation.3 | async-start | bytes 2048 | tf_op jit(solution)/shard_map/slice | solution.py:199
  95.4 12.9 %collective-permute-start.16 = (f32[256]{0:T(256)S(1)}, f32[256]{0:T(256)S(1)}, u32[]{:S(2)}, u32[]{:S(2)}) collective-permute-start(f32[256]{0:T(256)S(1)} %subtract_exponential_fusion), channel_id=1, source_target_pairs={{0,128},{128,0},{1,129},{129,1},{2,130},{130,2},{3,131},{131,3},{4... | collective-permute-start | bytes 3080 | tf_op jit(solution)/shard_map/ppermute | solution.py:30
  98.6 40.7 %all-to-all-start.1 = ((bf16[16,16,4096]{2,1,0:T(8,128)(2,1)}), bf16[16,16,4096]{2,1,0:T(8,128)(2,1)S(1)}, u32[]{:S(2)}, u32[]{:S(2)}) async-start(bf16[16,16,4096]{2,1,0:T(8,128)(2,1)} %bitcast.13), calls=%async_computation.1 | async-start | bytes 4194304 | tf_op jit(solution)/shard_map/all_to_all | solution.py:205
  125.7 3.5 %collective-permute-start.20 = (bf16[256,2048]{1,0:T(8,128)(2,1)}, bf16[256,2048]{1,0:T(8,128)(2,1)S(1)}, u32[]{:S(2)}, u32[]{:S(2)}) collective-permute-start(bf16[256,2048]{1,0:T(8,128)(2,1)} %get-tuple-element.47), channel_id=1, source_target_pairs={{0,32},{32,0},{1,33},{33,1},{2,34},{34,2},{3,35},{35,3},{4,36},{36... | collective-permute-start | bytes 3145736 | tf_op jit(solution)/shard_map/ppermute | solution.py:30
  125.7 14.0 %collective-permute-start.18 = (bf16[256,2048]{1,0:T(8,128)(2,1)}, bf16[256,2048]{1,0:T(8,128)(2,1)}, u32[]{:S(2)}, u32[]{:S(2)}) collective-permute-start(bf16[256,2048]{1,0:T(8,128)(2,1)} %get-tuple-element.44), channel_id=1, source_target_pairs={{0,32},{32,0},{1,33},{33,1},{2,34},{34,2},{3,35},{35,3},{4,36},{36... | collective-permute-start | bytes 3145736 | tf_op jit(solution)/shard_map/ppermute | solution.py:30
  131.3 38.5 %collective-permute-start.21 = (bf16[128,2048]{1,0:T(8,128)(2,1)}, bf16[128,2048]{1,0:T(8,128)(2,1)}, u32[]{:S(2)}, u32[]{:S(2)}) collective-permute-start(bf16[128,2048]{1,0:T(8,128)(2,1)} %add_convert_fusion), channel_id=1, source_target_pairs={{0,64},{64,0},{1,65},{65,1},{2,66},{66,2},{3,67},{67,3},{4,68},{68... | collective-permute-start | bytes 1572872 | tf_op jit(solution)/shard_map/ppermute | solution.py:30
  139.3 1.6 copy-start.3
  139.6 17.8 %collective-permute-start.22 = (f32[8,4096]{1,0:T(8,128)S(1)}, f32[8,4096]{1,0:T(8,128)S(1)}, u32[]{:S(2)}, u32[]{:S(2)}) collective-permute-start(f32[8,4096]{1,0:T(8,128)S(1)} %slice_bitcast_fusion), channel_id=1, source_target_pairs={{0,1},{1,0},{2,3},{3,2},{4,5},{5,4},{6,7},{7,6},{8,9},{9,8},{10,11... | collective-permute-start | bytes 393224 | tf_op jit(solution)/shard_map/ppermute | solution.py:30
  142.0 27.8 %copy-start.2 = (f32[256,2048]{1,0:T(8,128)S(1)}, f32[256,2048]{1,0:T(8,128)}, u32[]{:S(2)}) copy-start(f32[256,2048]{1,0:T(8,128)} %get-tuple-element.46) | copy-start | bytes 6291460
  142.0 26.5 %collective-permute-start.19 = (bf16[128,2048]{1,0:T(8,128)(2,1)S(1)}, bf16[128,2048]{1,0:T(8,128)(2,1)S(1)}, u32[]{:S(2)}, u32[]{:S(2)}) collective-permute-start(bf16[128,2048]{1,0:T(8,128)(2,1)S(1)} %add_convert_fusion.1), channel_id=1, source_target_pairs={{0,64},{64,0},{1,65},{65,1},{2,66},{66,2},{3,67},{67,3},{4,68},{68... | collective-permute-start | bytes 1572872 | tf_op jit(solution)/shard_map/ppermute | solution.py:30
Sparse Core Ops, SparseCore 0:
  30.8 83.6 all-gather.1
